TPU v7x, 256 devices: a whole 4x4x8 slice. The times are simulated.
256 devices in a mesh: row: 8 (over z), col: 32 (over y, x, core).
Axes of the slice: x: 4, y: 4, z: 8, core: 2. Of those that a mesh axis runs over, the one named last changes fastest.
Arguments:
- ancestor_inverse: bfloat16 [24576, 24576], P('row', 'col'), may hold values from -6 to 6
- factor_slots: bfloat16 [3, 16384, 512], P(None, ('row', 'col')), may hold values from -0.25 to 0.25
- slot_tiles: int32 [3, 64], replicated, may hold values from -1 to 95, as said below
- parent_factor: bfloat16 [2, 512, 512], replicated, may hold values from -0.25 to 0.25
- diag_inverse: float32 [3, 512, 512], replicated, may hold values from -6 to 6
Outputs:
- inverse_panels: bfloat16 [3, 24576, 512], P(None, ('row', 'col'))
- diag_blocks: float32 [3, 512, 512], replicated
- parent_blocks: float32 [2, 512, 512], replicated
Inputs may be any that keep to these rules, and one draw needn't show every extreme that they name: `slot_tiles`: entries b * 2 to b * 2 + 1 of a supernode's row are the slots of column block b: each is -1 (empty) or names a tile from b * 3 to b * 3 + 2, no tile twice; in each supernode some block has all its slots filled. `factor_slots`: rows of an empty slot are not part of the factor.
All inputs are finite; a program needn't handle non-finite values.
Results may differ from a plain program's by a relative error of at most 0.00075.
Values may be sent and summed in bfloat16 or wider, within the bound.
No kernel may reach another device: no remote copies, remote signals or barrier semaphores. Data moves between devices by JAX's collectives and lax.ppermute only.
A program may use at most 128 MiB of HBM per device.

v0:
```python
import jax
import jax.numpy as jnp
from jax import lax
from jax.experimental import pallas as pl
from jax.experimental.pallas import tpu as pltpu
from jax.sharding import Mesh, PartitionSpec as P


AXES = ("z", "y", "x", "k")
SIZES = (8, 4, 4, 2)
CAP = 2
TPC = 3


def number(z, y, x, k):
    return ((z % 8 * 4 + y % 4) * 4 + x % 4) * 2 + k % 2


def hop(value, move):
    pairs = []
    for z in range(8):
        for y in range(4):
            for x in range(4):
                for k in range(2):
                    pairs.append((number(z, y, x, k), number(*move(z, y, x, k))))
    return lax.ppermute(value, AXES, pairs)


def swap_cores(value):
    return hop(value, lambda z, y, x, k: (z, y, x, k + 1))


def step_x(value, by):
    return hop(value, lambda z, y, x, k: (z, y, x + by, k))


def step_first(value, by):
    return hop(value, lambda z, y, x, k: (z, y + by * k, x + by * (1 - k), k))


def step_second(value, by):
    return hop(value, lambda z, y, x, k: (z, y + by * (1 - k), x + by * k, k))


def step_z(value, by):
    return hop(value, lambda z, y, x, k: (z + by, y, x, k))


def to_column(value):
    count = 256
    pairs = [(b * 8 + j, j * 32 + b) for b in range(count // 8) for j in range(8)]
    return lax.ppermute(value, AXES, pairs)


def after(value, other):
    return lax.optimization_barrier((value, other))[0]


def picked(value, index, axis):
    return lax.dynamic_index_in_dim(value, index, axis, keepdims=False)


def two_parts(value):
    high = value.astype(jnp.bfloat16)
    return high, (value - high.astype(jnp.float32)).astype(jnp.bfloat16)


def times_split(value, matrix):
    rows = value.shape[0]
    out = jnp.dot(
        jnp.concatenate(two_parts(value), axis=0), matrix, preferred_element_type=jnp.float32
    )
    return out[:rows] + out[rows:]


def transposed_times(matrix, value):
    cols = value.shape[1]
    out = lax.dot_general(
        matrix,
        jnp.concatenate(two_parts(value), axis=1),
        (((0,), (0,)), ((), ())),
        preferred_element_type=jnp.float32,
    )
    return out[:, :cols] + out[:, cols:]


def stacked(pieces):
    count = len(pieces)

    def kernel(*refs):
        for i in range(count):
            refs[count][i] = refs[i][...]

    return pl.pallas_call(
        kernel, out_shape=jax.ShapeDtypeStruct((count,) + pieces[0].shape, pieces[0].dtype)
    )(*pieces)


def products(place, tiles, split_rows, handed, own_pieces, other_pieces, offsets, base):
    _, _, _, panel_rows, block_cols = split_rows.shape
    node_count, piece_rows, width = own_pieces[0].shape
    tile_rows = block_cols // TPC
    half = width // 2
    per_slot = tile_rows // piece_rows
    spans = len(offsets)

    def offset_of(i):
        where = jnp.int32(offsets[0])
        for at in range(1, spans):
            where = jnp.where(i == at, offsets[at], where)
        return where

    def kernel(place, tiles, *refs):
        columns = (refs[0:4], refs[4:8])
        pieces = (refs[8:16], refs[16:24])
        outs = refs[24:-1]
        slots = refs[-1]
        node = pl.program_id(1)
        z = place[0]
        first = (place[1] * 4 + place[2]) * 2
        sums = [None, None]
        for side, block in ((0, first + place[3]), (1, first + 1 - place[3])):
            for i in range(8):
                piece = pieces[side][i][...].reshape(piece_rows, width)
                slots[side, lax.rem(z + i + 4, 8)] = piece
            for member in range(CAP):
                name = tiles[base + node, block * CAP + member]
                tile = jnp.clip(name - block * TPC, 0, TPC - 1)
                at = pl.ds(pl.multiple_of(tile * tile_rows, tile_rows), tile_rows)
                rows = slots[side, member * per_slot : (member + 1) * per_slot]
                rows = rows.reshape(tile_rows, width)
                rows = jnp.where(name >= 0, rows, jnp.zeros_like(rows))
                left = jnp.concatenate(
                    [part[..., at].reshape(panel_rows, tile_rows) for part in columns[side]], axis=0
                )
                for i in range(2):
                    term = jnp.dot(
                        left, rows[:, i * half : (i + 1) * half], preferred_element_type=jnp.float32
                    )
                    sums[i] = term if sums[i] is None else sums[i] + term
        for at in range(spans):

            @pl.when(pl.program_id(0) == at)
            def _():
                outs[2 * at][...] = sums[0].reshape(4, panel_rows, half)
                outs[2 * at + 1][...] = sums[1].reshape(4, panel_rows, half)

    def at_chip(j, d, p):
        along_y = jnp.where(p[3] == 0, j, lax.rem(p[1] + offset_of(d), 4))
        along_x = jnp.where(p[3] == 0, lax.rem(p[2] + offset_of(d), 4), j)
        return along_y, along_x

    def kept_at(j):
        return lambda d, i, p, t: at_chip(j, d, p) + (p[3], 0, 0)

    def given_at(j):
        return lambda d, i, p, t: at_chip(j, d, p) + (0, 0)

    def out_at(at):
        return lambda d, i, p, t: (
            0,
            0,
            jnp.where(d == at, i, jnp.where(d < at, 0, node_count - 1)),
        )

    strip = (panel_rows, block_cols)
    out = jax.ShapeDtypeStruct((4, panel_rows, node_count * half), jnp.float32)
    return pl.pallas_call(
        kernel,
        grid_spec=pltpu.PrefetchScalarGridSpec(
            num_scalar_prefetch=2,
            grid=(spans, node_count),
            in_specs=[pl.BlockSpec((1, 1, 1) + strip, kept_at(j)) for j in range(4)]
            + [pl.BlockSpec((1, 1) + strip, given_at(j)) for j in range(4)]
            + [pl.BlockSpec((1, piece_rows, width), lambda d, i, p, t: (i, 0, 0))] * 16,
            out_specs=[
                pl.BlockSpec((4, panel_rows, half), out_at(at)) for at in range(spans) for _ in range(2)
            ],
            scratch_shapes=[pltpu.VMEM((2, 8, piece_rows, width), jnp.bfloat16)],
        ),
        out_shape=[out] * (2 * spans),
    )(place, tiles, *[split_rows] * 4, *[handed] * 4, *own_pieces, *other_pieces)


def chain(place, shares, links, node_count):
    panel_rows = shares[0][0][0].shape[0]
    counts = [low[0].shape[1] for low, _ in shares]
    half = sum(counts) // node_count
    width = 2 * half
    quarter = width // 4
    spots = [
        (run, slice(i * half, (i + 1) * half))
        for run, cols in enumerate(counts)
        for i in range(cols // half)
    ]
    given = 6 * len(shares)

    def kernel(place, *refs):
        links, panels = refs[given : given + 2]
        spread = refs[given + 2 : given + 6]
        columns = refs[given + 6]
        previous = None
        for node, (run, cut) in enumerate(spots):
            low = refs[6 * run : 6 * run + 3]
            high = refs[6 * run + 3 : 6 * run + 6]
            column = -jnp.concatenate(
                [
                    low[0][:, cut] + low[1][:, cut] + low[2][:, cut],
                    high[0][:, cut] + high[1][:, cut] + high[2][:, cut],
                ],
                axis=1,
            )
            if node > 0:
                column = column - times_split(previous, links[node - 1])
            panels[node] = column.astype(jnp.bfloat16)
            columns[node] = column
            previous = column
        for d in range(4):
            start = pl.multiple_of(lax.rem(place[2] + d, 4) * quarter, quarter)
            spread[d][...] = columns[:, :, pl.ds(start, quarter)]

    vmem = pl.BlockSpec(memory_space=pltpu.VMEM)
    smem = pl.BlockSpec(memory_space=pltpu.SMEM)
    part = jax.ShapeDtypeStruct((node_count, panel_rows, quarter), jnp.float32)
    flat = [array for low, high in shares for array in tuple(low) + tuple(high)]
    outs = pl.pallas_call(
        kernel,
        in_specs=[smem] + [vmem] * (given + 1),
        out_specs=[vmem] * 5,
        out_shape=[jax.ShapeDtypeStruct((node_count, panel_rows, width), jnp.bfloat16)] + [part] * 4,
        scratch_shapes=[pltpu.VMEM((node_count, panel_rows, width), jnp.float32)],
        name="chain",
    )(place, *flat, links)
    return outs[0], outs[1:]


def contraction(place, tiles, block_panels, near, near_other):
    node_count, panel_rows, quarter = block_panels[0].shape
    _, _, piece_rows, width = near.shape
    half = width // 2
    granule = panel_rows // 3
    per_tile = piece_rows * 8 // CAP // granule
    per_piece = piece_rows // granule
    count = 2 * node_count - 1
    strip = half // 32

    def kernel(place, tiles, *refs):
        block_panels = refs[:4]
        near, near_other, keep, send, sums = refs[4:]
        x = place[2]
        k = place[3]
        block = place[0] * 4 + place[1]
        parts = []
        for node in range(node_count):
            first = tiles[node, block * CAP] - block * TPC
            second = tiles[node, block * CAP + 1] - block * TPC
            rows = []
            for d in range(4):
                part = lax.rem(x - d + 4, 4)
                for i in range(3):
                    at = 3 * (2 * part + k) + i
                    tile = at // per_tile
                    inner = at - tile * per_tile
                    in_second = second == tile
                    live = jnp.logical_or(first == tile, in_second)
                    piece = jnp.where(in_second, 8 // CAP, 0) + inner // per_piece
                    start = pl.multiple_of(lax.rem(inner, per_piece) * granule, granule)
                    along = lax.rem(piece // 2 - x + 4, 4)
                    value = jnp.where(
                        lax.rem(piece, 2) == k,
                        near[along, node, pl.ds(start, granule), :],
                        near_other[along, node, pl.ds(start, granule), :],
                    )
                    rows.append(jnp.where(live, value, jnp.zeros_like(value)))
            dense = jnp.concatenate(rows, axis=0)
            parts.append(two_parts(jnp.concatenate([p[node] for p in block_panels], axis=0)))
            right = parts[node] if node == 0 else parts[node] + parts[node - 1]
            out = lax.dot_general(
                dense,
                jnp.concatenate(right, axis=1),
                (((0,), (0,)), ((), ())),
                preferred_element_type=jnp.float32,
            )
            cols = [out[:, i * quarter : (i + 1) * quarter] for i in range(len(right))]
            sums[node] = cols[0] + cols[1]
            if node > 0:
                sums[node_count + node - 1] = cols[2] + cols[3]
        mine = pl.multiple_of(k * half, half)
        theirs = pl.multiple_of((1 - k) * half, half)
        for i in range(count):
            stay = sums[i, pl.ds(mine, half), :].reshape(8, 4, strip, quarter)
            leave = sums[i, pl.ds(theirs, half), :].reshape(8, 4, strip, quarter)
            for y in range(4):
                keep[y, :, i] = stay[:, y]
                send[y, :, i] = leave[:, y]

    out = jax.ShapeDtypeStruct((4, 8, count, strip, quarter), jnp.float32)
    vmem = pl.BlockSpec(memory_space=pltpu.VMEM)
    smem = pl.BlockSpec(memory_space=pltpu.SMEM)
    return pl.pallas_call(
        kernel,
        in_specs=[smem, smem] + [vmem] * 6,
        out_specs=[vmem, vmem],
        out_shape=[out, out],
        scratch_shapes=[pltpu.VMEM((count, width, quarter), jnp.float32)],
        name="contraction",
    )(place, tiles, *block_panels, near, near_other)


def tail(place, plane, other, links, diag_inverse):
    _, _, count, strip, quarter = plane.shape
    node_count, width, _ = diag_inverse.shape

    def kernel(place, plane, other, links, diag_inverse, diagonals, parents, sums):
        k = place[3]

        def place_sum(i, carry):
            for source, side in ((plane, k), (other, 1 - k)):
                for y in range(4):
                    for x in range(4):
                        sums[i, side, :, y, :, x * quarter : (x + 1) * quarter] = source[
                            y * 4 + x, :, i
                        ]
            return carry

        lax.fori_loop(0, count, place_sum, 0)
        diagonals[0] = diag_inverse[0] - sums[0].reshape(width, width)

        def finish(node, carry):
            link = links[node - 1]
            second = sums[node_count + node - 1].reshape(width, width).T
            upper = -(second + times_split(diagonals[node - 1], link))
            parents[node - 1] = upper
            first = sums[node].reshape(width, width)
            diagonals[node] = diag_inverse[node] - first - transposed_times(link, upper)
            return carry

        lax.fori_loop(1, node_count, finish, 0)

    vmem = pl.BlockSpec(memory_space=pltpu.VMEM)
    smem = pl.BlockSpec(memory_space=pltpu.SMEM)
    return pl.pallas_call(
        kernel,
        in_specs=[smem, vmem, vmem, vmem, vmem],
        out_specs=[vmem, vmem],
        out_shape=[
            jax.ShapeDtypeStruct((node_count, width, width), jnp.float32),
            jax.ShapeDtypeStruct((node_count - 1, width, width), jnp.float32),
        ],
        scratch_shapes=[pltpu.VMEM((count, 2, 8, 4, strip, width), jnp.float32)],
        name="tail",
    )(place, plane, other, links, diag_inverse)


def ring_sum(own, behind, middle, ahead, step):
    far_low = step(middle[0], -1)
    far_high = step(middle[1], 1)
    raw_low = step(ahead[0], 1)
    raw_high = step(behind[1], -1)
    joined_low = behind[0] + far_low
    joined_high = ahead[1] + far_high
    low = (own[0], raw_low, step(joined_low, -1))
    high = (own[1], raw_high, step(joined_high, 1))
    return low, high


def on_device(ancestor_inverse, factor_slots, slot_tiles, parent_factor, diag_inverse):
    z = lax.axis_index("z")
    y = lax.axis_index("y")
    x = lax.axis_index("x")
    k = lax.axis_index("k")
    place = jnp.stack([z, y, x, k]).astype(jnp.int32)
    block_rows, block_cols = ancestor_inverse.shape
    node_count, _, _ = factor_slots.shape
    panel_rows = block_rows // 32

    split_rows = ancestor_inverse.reshape(4, 4, 2, panel_rows, block_cols)
    leaving = picked(split_rows, 1 - k, 2)
    next_x = step_x(factor_slots, -1)
    last_x = step_x(factor_slots, 1)
    first_piece, leaving, next_x, last_x = lax.optimization_barrier(
        (to_column(factor_slots), leaving, next_x, last_x)
    )
    handed = swap_cores(leaving)
    far_x = hop(
        jnp.where(k == 0, next_x, last_x), lambda z, y, x, k: (z, y, x + 2 * k - 1, k)
    )
    near = [factor_slots, next_x, far_x, last_x]

    behind = []
    ahead = []
    other_behind = []
    other_ahead = []
    moving_up = moving_down = first_piece
    other_first = swap_cores(first_piece)
    for i in range(4):
        if i == 2:
            moving_up, other_first = lax.optimization_barrier((moving_up, other_first))
        if i == 3:
            moving_up, other_behind[0], other_ahead[0], handed, *near = lax.optimization_barrier(
                (moving_up, other_behind[0], other_ahead[0], handed, *near)
            )
        moving_up = step_z(moving_up, 1)
        behind.append(moving_up)
        other_behind.append(swap_cores(moving_up))
        if i < 3:
            moving_down = step_z(moving_down, -1)
            ahead.append(moving_down)
            other_ahead.append(swap_cores(moving_down))
    own_pieces = behind[::-1] + [first_piece] + ahead
    other_pieces = other_behind[::-1] + [other_first] + other_ahead

    def shares(offsets, place):
        return products(
            place, slot_tiles, split_rows, handed, own_pieces, other_pieces, offsets, 0
        )

    middle = shares((2,), place)
    raw = shares((3, 1), after(place, middle[0]))
    own = shares((0,), after(place, raw[0]))
    near[0] = after(near[0], own[0])
    near = stacked(near)
    near_other = swap_cores(near)
    low, high = ring_sum(own, raw[0:2], middle, raw[2:4], step_first)
    here, near, near_other = lax.optimization_barrier((jnp.where(k == 0, y, x), near, near_other))

    def regroup(offset, here):
        at = (here + offset) % 4
        return [sum(picked(share, at, 0) for share in group) for group in (low, high)]

    far = regroup(2, here)
    here, *far = lax.optimization_barrier((here, *far))
    ahead_share, behind_share = regroup(1, here), regroup(3, here)
    here, *raw = lax.optimization_barrier((here, ahead_share[0], behind_share[1]))
    ahead_share[0], behind_share[1] = raw
    own_share = regroup(0, here)
    low, high = ring_sum(own_share, behind_share, far, ahead_share, step_second)
    panels, spread = chain(place, [(low, high)], parent_factor, node_count)

    block_panels = [spread[0]] + [step_x(spread[d], d) for d in range(1, 4)]
    keep, send = contraction(place, slot_tiles, block_panels, near, near_other)
    sums = jnp.sum(lax.all_to_all(keep + swap_cores(send), "y", 0, 0, tiled=True), axis=0)
    sums = jnp.sum(lax.all_to_all(sums, "z", 0, 0, tiled=True), axis=0)
    over_z = lax.all_to_all(jnp.broadcast_to(sums, (8,) + sums.shape), "z", 0, 0, tiled=True)
    plane = lax.all_to_all(
        jnp.broadcast_to(over_z, (16,) + over_z.shape), ("y", "x"), 0, 0, tiled=True
    )
    diagonals, parents = tail(place, plane, swap_cores(plane), parent_factor, diag_inverse)
    return panels, diagonals, parents


def solution(mesh):
    grid = Mesh(mesh.devices.reshape(SIZES), AXES)
    placed = (P("z", ("y", "x", "k")), P(None, AXES, None), P(), P(), P())
    return jax.shard_map(
        on_device,
        mesh=grid,
        in_specs=placed,
        out_specs=(P(None, AXES, None), P(), P()),
        check_vma=False,
    )
```

profile of v0, /device:TPU:8, one launch (start us, length us, event | category | flops | bytes accessed | tf_op | source)
XLA Modules:
  0.0 251.2 jit_solution(5472698137346208849)
XLA Ops:
  0.6 2.8 %collective-permute-start.1 = (bf16[3,64,512]{2,1,0:T(8,128)(2,1)}, bf16[3,64,512]{2,1,0:T(8,128)(2,1)S(1)}, u32[]{:S(2)}, u32[]{:S(2)}) collective-permute-start(bf16[3,64,512]{2,1,0:T(8,128)(2,1)} %refs_0_), channel_id=1, source_target_pairs={{0,6},{1,7},{2,0},{3,1},{4,2},{5,3},{6,4},{7,5},{8,14},{9,15},{10,... | collective-permute-start | bytes 589832 | tf_op jit(solution)/shard_map/ppermute | solution.py:26
  3.5 1.9 collective-permute-start
  5.4 3.8 %collective-permute-start.2 = (bf16[3,64,512]{2,1,0:T(8,128)(2,1)}, bf16[3,64,512]{2,1,0:T(8,128)(2,1)}, u32[]{:S(2)}, u32[]{:S(2)}) collective-permute-start(bf16[3,64,512]{2,1,0:T(8,128)(2,1)} %refs_0_), channel_id=1, source_target_pairs={{0,2},{1,3},{2,4},{3,5},{4,6},{5,7},{6,0},{7,1},{8,10},{9,11},{10,... | collective-permute-start | bytes 589832 | tf_op jit(solution)/shard_map/ppermute | solution.py:26
  9.2 3.2 %dynamic-slice_bitcast_fusion = bf16[4,4,96,768]{3,2,1,0:T(8,128)(2,1)} fusion(bf16[4,4,2,96,768]{4,3,2,1,0:T(8,128)(2,1)} %bitcast.23, s32[]{:T(128)S(6)} %select_n.67), kind=kLoop, calls=%fused_computation | loop fusion | bytes 4718596 | tf_op jit(solution)/shard_map/jit(dynamic_index_in_dim)/squeeze | solution.py:60
  12.5 11.0 %collective-permute-done.refs_12_ = bf16[3,64,512]{2,1,0:T(8,128)(2,1)S(1)} collective-permute-done((bf16[3,64,512]{2,1,0:T(8,128)(2,1)}, bf16[3,64,512]{2,1,0:T(8,128)(2,1)S(1)}, u32[]{:S(2)}, u32[]{:S(2)}) %collective-permute-start) | collective-permute-done | bytes 196640 | tf_op jit(solution)/shard_map/ppermute | solution.py:52
  24.0 3.7 %collective-permute-start.8 = (bf16[3,64,512]{2,1,0:T(8,128)(2,1)S(1)}, bf16[3,64,512]{2,1,0:T(8,128)(2,1)S(1)}, u32[]{:S(2)}, u32[]{:S(2)}) collective-permute-start(bf16[3,64,512]{2,1,0:T(8,128)(2,1)S(1)} %collective-permute-done.refs_12_), channel_id=1, source_target_pairs={{0,224},{1,225},{2,226},{3,227},{4,228},{5,229},{6,230},{7,231},{8... | collective-permute-start | bytes 589832 | tf_op jit(solution)/shard_map/ppermute | solution.py:26
  27.9 5.3 %collective-permute-done.3.refs_11_ = bf16[3,64,512]{2,1,0:T(8,128)(2,1)S(1)} collective-permute-done((bf16[3,64,512]{2,1,0:T(8,128)(2,1)S(1)}, bf16[3,64,512]{2,1,0:T(8,128)(2,1)S(1)}, u32[]{:S(2)}, u32[]{:S(2)}) %collective-permute-start.3) | collective-permute-done | bytes 196640 | tf_op jit(solution)/shard_map/ppermute | solution.py:26
  34.1 3.3 %collective-permute-start.13 = (bf16[3,64,512]{2,1,0:T(8,128)(2,1)S(1)}, bf16[3,64,512]{2,1,0:T(8,128)(2,1)S(1)}, u32[]{:S(2)}, u32[]{:S(2)}) collective-permute-start(bf16[3,64,512]{2,1,0:T(8,128)(2,1)S(1)} %collective-permute-done.8.refs_13_), channel_id=1, source_target_pairs={{0,224},{1,225},{2,226},{3,227},{4,228},{5,229},{6,230},{7,231},{8... | collective-permute-start | bytes 589832 | tf_op jit(solution)/shard_map/ppermute | solution.py:26
  37.4 4.0 %collective-permute-done.4.refs_10_ = bf16[3,64,512]{2,1,0:T(8,128)(2,1)S(1)} collective-permute-done((bf16[3,64,512]{2,1,0:T(8,128)(2,1)S(1)}, bf16[3,64,512]{2,1,0:T(8,128)(2,1)S(1)}, u32[]{:S(2)}, u32[]{:S(2)}) %collective-permute-start.4) | collective-permute-done | bytes 196640 | tf_op jit(solution)/shard_map/ppermute | solution.py:26
  41.9 3.7 %collective-permute-start.14 = (bf16[3,64,512]{2,1,0:T(8,128)(2,1)S(1)}, bf16[3,64,512]{2,1,0:T(8,128)(2,1)}, u32[]{:S(2)}, u32[]{:S(2)}) collective-permute-start(bf16[3,64,512]{2,1,0:T(8,128)(2,1)S(1)} %collective-permute-done.13.refs_14_), channel_id=1, source_target_pairs={{0,224},{1,225},{2,226},{3,227},{4,228},{5,229},{6,230},{7,231},{8... | collective-permute-start | bytes 589832 | tf_op jit(solution)/shard_map/ppermute | solution.py:26
  45.6 4.4 %collective-permute-done.6.refs_9_ = bf16[3,64,512]{2,1,0:T(8,128)(2,1)} collective-permute-done((bf16[3,64,512]{2,1,0:T(8,128)(2,1)S(1)}, bf16[3,64,512]{2,1,0:T(8,128)(2,1)}, u32[]{:S(2)}, u32[]{:S(2)}) %collective-permute-start.6) | collective-permute-done | bytes 196640 | tf_op jit(solution)/shard_map/ppermute | solution.py:26
  51.2 6.8 %collective-permute-done.12.refs_8_ = bf16[3,64,512]{2,1,0:T(8,128)(2,1)} collective-permute-done((bf16[3,64,512]{2,1,0:T(8,128)(2,1)}, bf16[3,64,512]{2,1,0:T(8,128)(2,1)}, u32[]{:S(2)}, u32[]{:S(2)}) %collective-permute-start.12) | collective-permute-done | bytes 196640 | tf_op jit(solution)/shard_map/ppermute | solution.py:26
  59.8 6.3 %shard_map.76 = (f32[4,96,768]{2,1,0:T(8,128)}, f32[4,96,768]{2,1,0:T(8,128)}) custom-call(s32[4]{0:T(128)} %pad_add_fusion.place, s32[3,64]{1,0:T(4,128)} %tiles.7, bf16[4,4,2,96,768]{4,3,2,1,0:T(8,128)(2,1)} %bitcast.24, bf16[4,4,2,96,768]{4,3,2,1,0:T(8,128)(2,1)} %bitcast.25, bf16[4,4,2,96,768]{4,3,2,1,0:T(8,128)(2,1)} %bitcast.26, ...), custom_call_target="tpu_custom_call" | custom-call | tf_op jit(solution)/shard_map/pallas_call | solution.py:168
  66.3 1.9 collective-permute-start.25
  68.2 10.0 %shard_map.77 = (f32[4,96,768]{2,1,0:T(8,128)}, f32[4,96,768]{2,1,0:T(8,128)}, f32[4,96,768]{2,1,0:T(8,128)}, f32[4,96,768]{2,1,0:T(8,128)}) custom-call(s32[4]{0:T(128)} %pad_add_fusion.place, s32[3,64]{1,0:T(4,128)} %tiles.7, bf16[4,4,2,96,768]{4,3,2,1,0:T(8,128)(2,1)} %bitcast.28, bf16[4,4,2,96,768]{4,3,2,1,0:T(8,128)(2,1)} %bitcast.29, ...), custom_call_target="tpu_custom_call" | custom-call | tf_op jit(solution)/shard_map/pallas_call | solution.py:168
  78.4 4.1 %collective-permute-done.22 = f32[4,96,768]{2,1,0:T(8,128)S(1)} collective-permute-done((f32[4,96,768]{2,1,0:T(8,128)}, f32[4,96,768]{2,1,0:T(8,128)S(1)}, u32[]{:S(2)}, u32[]{:S(2)}) %collective-permute-start.22) | collective-permute-done | bytes 1179680 | tf_op jit(solution)/shard_map/ppermute | solution.py:26
  82.6 1.5 add.158
  85.8 2.0 collective-permute-start.26
  87.8 6.2 %shard_map.78 = (f32[4,96,768]{2,1,0:T(8,128)}, f32[4,96,768]{2,1,0:T(8,128)}) custom-call(s32[4]{0:T(128)} %pad_add_fusion.place, s32[3,64]{1,0:T(4,128)} %tiles.7, bf16[4,4,2,96,768]{4,3,2,1,0:T(8,128)(2,1)} %bitcast.32, bf16[4,4,2,96,768]{4,3,2,1,0:T(8,128)(2,1)} %bitcast.33, bf16[4,4,2,96,768]{4,3,2,1,0:T(8,128)(2,1)} %bitcast.34, ...), custom_call_target="tpu_custom_call" | custom-call | tf_op jit(solution)/shard_map/pallas_call | solution.py:168
  93.9 2.2 shard_map.79.refs_4_
  96.1 2.6 %collective-permute-done.20.refs_5_ = bf16[4,3,64,512]{3,2,1,0:T(8,128)(2,1)} collective-permute-done((bf16[4,3,64,512]{3,2,1,0:T(8,128)(2,1)}, bf16[4,3,64,512]{3,2,1,0:T(8,128)(2,1)}, u32[]{:S(2)}, u32[]{:S(2)}) %collective-permute-start.20) | collective-permute-done | bytes 786464 | tf_op jit(solution)/shard_map/ppermute | solution.py:26
  98.7 1.7 collective-permute-done.23
  100.5 2.0 add_bitcast_fusion.5
  102.5 10.6 %collective-permute-done.24 = f32[4,96,768]{2,1,0:T(8,128)} collective-permute-done((f32[4,96,768]{2,1,0:T(8,128)}, f32[4,96,768]{2,1,0:T(8,128)}, u32[]{:S(2)}, u32[]{:S(2)}) %collective-permute-start.24) | collective-permute-done | bytes 1179680 | tf_op jit(solution)/shard_map/ppermute | solution.py:26
  113.1 1.9 add_bitcast_fusion.4
  115.0 2.4 collective-permute-start.28
  117.4 1.8 add_bitcast_fusion.3
  119.2 1.7 add_bitcast_fusion.2
  120.9 1.9 collective-permute-start.27
  123.1 1.9 bitcast_add_fusion.1
  125.0 3.2 %collective-permute-start.29 = (f32[96,768]{1,0:T(8,128)}, f32[96,768]{1,0:T(8,128)}, u32[]{:S(2)}, u32[]{:S(2)}) collective-permute-start(f32[96,768]{1,0:T(8,128)} %bitcast_add_fusion.1), channel_id=1, source_target_pairs={{0,24},{1,7},{2,26},{3,1},{4,28},{5,3},{6,30},{7,5},{8,0},{9,15},{... | collective-permute-start | bytes 884744 | tf_op jit(solution)/shard_map/ppermute | solution.py:26
  128.2 1.8 bitcast_add_fusion
  130.1 2.1 add_bitcast_fusion
  132.1 1.7 collective-permute-done.29.refs_2_
  133.9 3.2 %collective-permute-done.32.refs_5_ = f32[96,768]{1,0:T(8,128)} collective-permute-done((f32[96,768]{1,0:T(8,128)}, f32[96,768]{1,0:T(8,128)}, u32[]{:S(2)}, u32[]{:S(2)}) %collective-permute-start.32) | collective-permute-done | bytes 294944 | tf_op jit(solution)/shard_map/ppermute | solution.py:26
  137.1 3.3 %chain.1 = (bf16[3,96,512]{2,1,0:T(8,128)(2,1)}, f32[3,96,128]{2,1,0:T(8,128)}, f32[3,96,128]{2,1,0:T(8,128)}, f32[3,96,128]{2,1,0:T(8,128)}, f32[3,96,128]{2,1,0:T(8,128)}) custom-call(s32[4]{0:T(128)} %pad_add_fusion.place, f32[96,768]{1,0:T(8,128)} %get-tuple-element.90.refs_0_, f32[96,768]{1,0:T(8,128)} %collective-permute-done.27.refs_1_, ...), custom_call_target="tpu_custom_call" | custom-call | tf_op jit(solution)/shard_map/chain/pallas_call | solution.py:226
  140.4 1.9 collective-permute-start.33
  142.3 3.3 %collective-permute-start.34 = (f32[3,96,128]{2,1,0:T(8,128)}, f32[3,96,128]{2,1,0:T(8,128)S(1)}, u32[]{:S(2)}, u32[]{:S(2)}) collective-permute-start(f32[3,96,128]{2,1,0:T(8,128)} %get-tuple-element.81), channel_id=1, source_target_pairs={{0,4},{1,5},{2,6},{3,7},{4,0},{5,1},{6,2},{7,3},{8,12},{9,13},{10,... | collective-permute-start | bytes 442376 | tf_op jit(solution)/shard_map/ppermute | solution.py:26
  145.5 1.9 collective-permute-done.33.refs_1_
  147.4 3.0 %collective-permute-done.34.refs_2_ = f32[3,96,128]{2,1,0:T(8,128)S(1)} collective-permute-done((f32[3,96,128]{2,1,0:T(8,128)}, f32[3,96,128]{2,1,0:T(8,128)S(1)}, u32[]{:S(2)}, u32[]{:S(2)}) %collective-permute-start.34) | collective-permute-done | bytes 147488 | tf_op jit(solution)/shard_map/ppermute | solution.py:26
  151.6 3.9 %contraction.1 = (f32[4,8,5,8,128]{4,3,2,1,0:T(8,128)}, f32[4,8,5,8,128]{4,3,2,1,0:T(8,128)}) custom-call(s32[4]{0:T(128)} %pad_add_fusion.place, s32[3,64]{1,0:T(4,128)} %tiles.7, f32[3,96,128]{2,1,0:T(8,128)} %get-tuple-element.79.refs_0_, f32[3,96,128]{2,1,0:T(8,128)} %copy-done.15, f32[3,96,128]{2,1,0:T(8,128)} %copy-done.16, f32[3,96,128]{2,1,0:T(8,128)} %copy-done.17, ...), custom_call_target="tpu_custom_call" | custom-call | tf_op jit(solution)/shard_map/contraction/pallas_call | solution.py:300
  155.5 2.3 collective-permute-done.36
  159.0 15.6 %all_to_all.20 = f32[4,8,5,8,128]{4,3,2,1,0:T(8,128)S(1)} all-to-all(f32[4,8,5,8,128]{4,3,2,1,0:T(8,128)S(1)} %add.193), channel_id=1, replica_groups=mesh['z'=8,'y'=4,'x'=4,'k'=2] {'y'}, dimensions={0} | all-to-all | bytes 1310720 | tf_op jit(solution)/shard_map/all_to_all | solution.py:442
  174.6 16.2 %all_to_all.21 = f32[8,5,8,128]{3,2,1,0:T(8,128)S(1)} all-to-all(f32[8,5,8,128]{3,2,1,0:T(8,128)S(1)} %reduce_sum.18), channel_id=1, replica_groups=mesh['z'=8,'y'=4,'x'=4,'k'=2] {'z'}, dimensions={0} | all-to-all | bytes 327680 | tf_op jit(solution)/shard_map/all_to_all | solution.py:443
  190.9 11.8 %all_to_all.22 = f32[8,5,8,128]{3,2,1,0:T(8,128)S(1)} all-to-all(f32[8,5,8,128]{3,2,1,0:T(8,128)S(1)} %broadcast_in_dim.6), channel_id=1, replica_groups=mesh['z'=8,'y'=4,'x'=4,'k'=2] {'z'}, dimensions={0} | all-to-all | bytes 327680 | tf_op jit(solution)/shard_map/all_to_all | solution.py:444
  203.0 34.5 %all_to_all.23.plane = f32[16,8,5,8,128]{4,3,2,1,0:T(8,128)S(1)} all-to-all(f32[16,8,5,8,128]{4,3,2,1,0:T(8,128)S(1)} %broadcast_in_dim.7), channel_id=1, replica_groups=mesh['z'=8,'y'=4,'x'=4,'k'=2] {'y','x'}, dimensions={0} | all-to-all | bytes 5242880 | tf_op jit(solution)/shard_map/all_to_all | solution.py:445
  237.5 5.0 %collective-permute-done.37.other = f32[16,8,5,8,128]{4,3,2,1,0:T(8,128)} collective-permute-done((f32[16,8,5,8,128]{4,3,2,1,0:T(8,128)S(1)}, f32[16,8,5,8,128]{4,3,2,1,0:T(8,128)}, u32[]{:S(2)}, u32[]{:S(2)}) %collective-permute-start.37) | collective-permute-done | bytes 2621472 | tf_op jit(solution)/shard_map/ppermute | solution.py:26
  242.5 8.7 %tail.1 = (f32[3,512,512]{2,1,0:T(8,128)}, f32[2,512,512]{2,1,0:T(8,128)}) custom-call(s32[4]{0:T(128)} %pad_add_fusion.place, f32[16,8,5,8,128]{4,3,2,1,0:T(8,128)} %copy-done.1, f32[16,8,5,8,128]{4,3,2,1,0:T(8,128)} %collective-permute-done.37.other, bf16[2,512,512]{2,1,0:T(8,128)(2,1)} %links.1, f32[3,512,512]{2,1,0:T(8,128)} %diag_inverse.1), custom_call_target="tpu_custom_call" | custom-call | tf_op jit(solution)/shard_map/tail/pallas_call | solution.py:342
  (92 shorter events, 10.0 us)
Async XLA Ops:
  0.6 11.8 %collective-permute-start.1 = (bf16[3,64,512]{2,1,0:T(8,128)(2,1)}, bf16[3,64,512]{2,1,0:T(8,128)(2,1)S(1)}, u32[]{:S(2)}, u32[]{:S(2)}) collective-permute-start(bf16[3,64,512]{2,1,0:T(8,128)(2,1)} %refs_0_), channel_id=1, source_target_pairs={{0,6},{1,7},{2,0},{3,1},{4,2},{5,3},{6,4},{7,5},{8,14},{9,15},{10,... | collective-permute-start | bytes 589832 | tf_op jit(solution)/shard_map/ppermute | solution.py:26
  3.5 20.0 %collective-permute-start = (bf16[3,64,512]{2,1,0:T(8,128)(2,1)}, bf16[3,64,512]{2,1,0:T(8,128)(2,1)S(1)}, u32[]{:S(2)}, u32[]{:S(2)}) collective-permute-start(bf16[3,64,512]{2,1,0:T(8,128)(2,1)} %refs_0_), channel_id=1, source_target_pairs={{0,0},{1,32},{2,64},{3,96},{4,128},{5,160},{6,192},{7,224},{8,1},{... | collective-permute-start | bytes 589832 | tf_op jit(solution)/shard_map/ppermute | solution.py:52
  5.4 18.1 %collective-permute-start.2 = (bf16[3,64,512]{2,1,0:T(8,128)(2,1)}, bf16[3,64,512]{2,1,0:T(8,128)(2,1)}, u32[]{:S(2)}, u32[]{:S(2)}) collective-permute-start(bf16[3,64,512]{2,1,0:T(8,128)(2,1)} %refs_0_), channel_id=1, source_target_pairs={{0,2},{1,3},{2,4},{3,5},{4,6},{5,7},{6,0},{7,1},{8,10},{9,11},{10,... | collective-permute-start | bytes 589832 | tf_op jit(solution)/shard_map/ppermute | solution.py:26
  12.5 21.6 %copy-start.13 = (bf16[3,64,512]{2,1,0:T(8,128)(2,1)}, bf16[3,64,512]{2,1,0:T(8,128)(2,1)S(1)}, u32[]{:S(2)}) copy-start(bf16[3,64,512]{2,1,0:T(8,128)(2,1)S(1)} %collective-permute-done.1.refs_1_) | copy-start | bytes 589828
  23.4 36.3 %copy-start.2 = (bf16[3,64,512]{2,1,0:T(8,128)(2,1)}, bf16[3,64,512]{2,1,0:T(8,128)(2,1)S(1)}, u32[]{:S(2)}) copy-start(bf16[3,64,512]{2,1,0:T(8,128)(2,1)S(1)} %collective-permute-done.refs_12_) | copy-start | bytes 589828
  23.4 26.6 %collective-permute-start.10 = (bf16[4,4,96,768]{3,2,1,0:T(8,128)(2,1)}, bf16[4,4,96,768]{3,2,1,0:T(8,128)(2,1)S(1)}, u32[]{:S(2)}, u32[]{:S(2)}) collective-permute-start(bf16[4,4,96,768]{3,2,1,0:T(8,128)(2,1)} %dynamic-slice_bitcast_fusion), channel_id=1, source_target_pairs={{0,1},{1,0},{2,3},{3,2},{4,5},{5,4},{6,7},{7,6},{8,9},{9,8},{10,11... | collective-permute-start | bytes 7077896 | tf_op jit(solution)/shard_map/ppermute | solution.py:26
  23.5 9.8 %collective-permute-start.3 = (bf16[3,64,512]{2,1,0:T(8,128)(2,1)S(1)}, bf16[3,64,512]{2,1,0:T(8,128)(2,1)S(1)}, u32[]{:S(2)}, u32[]{:S(2)}) collective-permute-start(bf16[3,64,512]{2,1,0:T(8,128)(2,1)S(1)} %collective-permute-done.refs_12_), channel_id=1, source_target_pairs={{0,32},{1,33},{2,34},{3,35},{4,36},{5,37},{6,38},{7,39},{8,40},{9,... | collective-permute-start | bytes 589832 | tf_op jit(solution)/shard_map/ppermute | solution.py:26
  24.0 10.1 %collective-permute-start.8 = (bf16[3,64,512]{2,1,0:T(8,128)(2,1)S(1)}, bf16[3,64,512]{2,1,0:T(8,128)(2,1)S(1)}, u32[]{:S(2)}, u32[]{:S(2)}) collective-permute-start(bf16[3,64,512]{2,1,0:T(8,128)(2,1)S(1)} %collective-permute-done.refs_12_), channel_id=1, source_target_pairs={{0,224},{1,225},{2,226},{3,227},{4,228},{5,229},{6,230},{7,231},{8... | collective-permute-start | bytes 589832 | tf_op jit(solution)/shard_map/ppermute | solution.py:26
  27.6 9.7 %collective-permute-start.5 = (bf16[3,64,512]{2,1,0:T(8,128)(2,1)S(1)}, bf16[3,64,512]{2,1,0:T(8,128)(2,1)S(1)}, u32[]{:S(2)}, u32[]{:S(2)}) collective-permute-start(bf16[3,64,512]{2,1,0:T(8,128)(2,1)S(1)} %collective-permute-done.refs_12_), channel_id=1, source_target_pairs={{0,1},{1,0},{2,3},{3,2},{4,5},{5,4},{6,7},{7,6},{8,9},{9,8},{10,11... | collective-permute-start | bytes 589832 | tf_op jit(solution)/shard_map/ppermute | solution.py:26
  33.2 26.5 %copy-start.3 = (bf16[3,64,512]{2,1,0:T(8,128)(2,1)}, bf16[3,64,512]{2,1,0:T(8,128)(2,1)S(1)}, u32[]{:S(2)}) copy-start(bf16[3,64,512]{2,1,0:T(8,128)(2,1)S(1)} %collective-permute-done.3.refs_11_) | copy-start | bytes 589828
  33.2 8.2 %collective-permute-start.4 = (bf16[3,64,512]{2,1,0:T(8,128)(2,1)S(1)}, bf16[3,64,512]{2,1,0:T(8,128)(2,1)S(1)}, u32[]{:S(2)}, u32[]{:S(2)}) collective-permute-start(bf16[3,64,512]{2,1,0:T(8,128)(2,1)S(1)} %collective-permute-done.3.refs_11_), channel_id=1, source_target_pairs={{0,32},{1,33},{2,34},{3,35},{4,36},{5,37},{6,38},{7,39},{8,40},{9,... | collective-permute-start | bytes 589832 | tf_op jit(solution)/shard_map/ppermute | solution.py:26
  33.2 8.2 %collective-permute-start.11 = (bf16[3,64,512]{2,1,0:T(8,128)(2,1)S(1)}, bf16[3,64,512]{2,1,0:T(8,128)(2,1)S(1)}, u32[]{:S(2)}, u32[]{:S(2)}) collective-permute-start(bf16[3,64,512]{2,1,0:T(8,128)(2,1)S(1)} %broadcast_select_fusion), channel_id=1, source_target_pairs={{0,6},{1,3},{2,0},{3,5},{4,2},{5,7},{6,4},{7,1},{8,14},{9,11},{10,... | collective-permute-start | bytes 589832 | tf_op jit(solution)/shard_map/ppermute | solution.py:26
  34.1 25.7 %copy-start.4 = (bf16[3,64,512]{2,1,0:T(8,128)(2,1)}, bf16[3,64,512]{2,1,0:T(8,128)(2,1)S(1)}, u32[]{:S(2)}) copy-start(bf16[3,64,512]{2,1,0:T(8,128)(2,1)S(1)} %collective-permute-done.8.refs_13_) | copy-start | bytes 589828
  34.1 7.8 %collective-permute-start.13 = (bf16[3,64,512]{2,1,0:T(8,128)(2,1)S(1)}, bf16[3,64,512]{2,1,0:T(8,128)(2,1)S(1)}, u32[]{:S(2)}, u32[]{:S(2)}) collective-permute-start(bf16[3,64,512]{2,1,0:T(8,128)(2,1)S(1)} %collective-permute-done.8.refs_13_), channel_id=1, source_target_pairs={{0,224},{1,225},{2,226},{3,227},{4,228},{5,229},{6,230},{7,231},{8... | collective-permute-start | bytes 589832 | tf_op jit(solution)/shard_map/ppermute | solution.py:26
  37.4 22.4 %copy-start.5 = (bf16[3,64,512]{2,1,0:T(8,128)(2,1)}, bf16[3,64,512]{2,1,0:T(8,128)(2,1)S(1)}, u32[]{:S(2)}) copy-start(bf16[3,64,512]{2,1,0:T(8,128)(2,1)S(1)} %collective-permute-done.5.refs_20_) | copy-start | bytes 589828
  37.4 8.2 %collective-permute-start.9 = (bf16[3,64,512]{2,1,0:T(8,128)(2,1)S(1)}, bf16[3,64,512]{2,1,0:T(8,128)(2,1)S(1)}, u32[]{:S(2)}, u32[]{:S(2)}) collective-permute-start(bf16[3,64,512]{2,1,0:T(8,128)(2,1)S(1)} %collective-permute-done.8.refs_13_), channel_id=1, source_target_pairs={{0,1},{1,0},{2,3},{3,2},{4,5},{5,4},{6,7},{7,6},{8,9},{9,8},{10,11... | collective-permute-start | bytes 589832 | tf_op jit(solution)/shard_map/ppermute | solution.py:26
  41.4 18.4 %copy-start.6 = (bf16[3,64,512]{2,1,0:T(8,128)(2,1)}, bf16[3,64,512]{2,1,0:T(8,128)(2,1)S(1)}, u32[]{:S(2)}) copy-start(bf16[3,64,512]{2,1,0:T(8,128)(2,1)S(1)} %collective-permute-done.4.refs_10_) | copy-start | bytes 589828
  41.4 4.2 %collective-permute-start.7 = (bf16[3,64,512]{2,1,0:T(8,128)(2,1)S(1)}, bf16[3,64,512]{2,1,0:T(8,128)(2,1)S(1)}, u32[]{:S(2)}, u32[]{:S(2)}) collective-permute-start(bf16[3,64,512]{2,1,0:T(8,128)(2,1)S(1)} %collective-permute-done.3.refs_11_), channel_id=1, source_target_pairs={{0,1},{1,0},{2,3},{3,2},{4,5},{5,4},{6,7},{7,6},{8,9},{9,8},{10,11... | collective-permute-start | bytes 589832 | tf_op jit(solution)/shard_map/ppermute | solution.py:26
  41.4 16.5 %copy-start.14 = (bf16[3,64,512]{2,1,0:T(8,128)(2,1)}, bf16[3,64,512]{2,1,0:T(8,128)(2,1)S(1)}, u32[]{:S(2)}) copy-start(bf16[3,64,512]{2,1,0:T(8,128)(2,1)S(1)} %collective-permute-done.11.refs_2_) | copy-start | bytes 589828
  41.4 8.6 %collective-permute-start.6 = (bf16[3,64,512]{2,1,0:T(8,128)(2,1)S(1)}, bf16[3,64,512]{2,1,0:T(8,128)(2,1)}, u32[]{:S(2)}, u32[]{:S(2)}) collective-permute-start(bf16[3,64,512]{2,1,0:T(8,128)(2,1)S(1)} %collective-permute-done.4.refs_10_), channel_id=1, source_target_pairs={{0,32},{1,33},{2,34},{3,35},{4,36},{5,37},{6,38},{7,39},{8,40},{9,... | collective-permute-start | bytes 589832 | tf_op jit(solution)/shard_map/ppermute | solution.py:26
  41.9 17.9 %copy-start.7 = (bf16[3,64,512]{2,1,0:T(8,128)(2,1)}, bf16[3,64,512]{2,1,0:T(8,128)(2,1)S(1)}, u32[]{:S(2)}) copy-start(bf16[3,64,512]{2,1,0:T(8,128)(2,1)S(1)} %collective-permute-done.13.refs_14_) | copy-start | bytes 589828
  41.9 8.9 %collective-permute-start.14 = (bf16[3,64,512]{2,1,0:T(8,128)(2,1)S(1)}, bf16[3,64,512]{2,1,0:T(8,128)(2,1)}, u32[]{:S(2)}, u32[]{:S(2)}) collective-permute-start(bf16[3,64,512]{2,1,0:T(8,128)(2,1)S(1)} %collective-permute-done.13.refs_14_), channel_id=1, source_target_pairs={{0,224},{1,225},{2,226},{3,227},{4,228},{5,229},{6,230},{7,231},{8... | collective-permute-start | bytes 589832 | tf_op jit(solution)/shard_map/ppermute | solution.py:26
  50.0 9.7 %copy-start = (bf16[4,4,96,768]{3,2,1,0:T(8,128)(2,1)}, bf16[4,4,96,768]{3,2,1,0:T(8,128)(2,1)S(1)}, u32[]{:S(2)}) copy-start(bf16[4,4,96,768]{3,2,1,0:T(8,128)(2,1)S(1)} %collective-permute-done.10.refs_4_.refs_5_.refs_6_.refs_7_) | copy-start | bytes 7077892
  50.0 7.9 %collective-permute-start.12 = (bf16[3,64,512]{2,1,0:T(8,128)(2,1)}, bf16[3,64,512]{2,1,0:T(8,128)(2,1)}, u32[]{:S(2)}, u32[]{:S(2)}) collective-permute-start(bf16[3,64,512]{2,1,0:T(8,128)(2,1)} %collective-permute-done.6.refs_9_), channel_id=1, source_target_pairs={{0,32},{1,33},{2,34},{3,35},{4,36},{5,37},{6,38},{7,39},{8,40},{9,... | collective-permute-start | bytes 589832 | tf_op jit(solution)/shard_map/ppermute | solution.py:26
  50.0 8.5 %collective-permute-start.18 = (bf16[3,64,512]{2,1,0:T(8,128)(2,1)S(1)}, bf16[3,64,512]{2,1,0:T(8,128)(2,1)}, u32[]{:S(2)}, u32[]{:S(2)}) collective-permute-start(bf16[3,64,512]{2,1,0:T(8,128)(2,1)S(1)} %collective-permute-done.13.refs_14_), channel_id=1, source_target_pairs={{0,1},{1,0},{2,3},{3,2},{4,5},{5,4},{6,7},{7,6},{8,9},{9,8},{10,11... | collective-permute-start | bytes 589832 | tf_op jit(solution)/shard_map/ppermute | solution.py:26
  50.1 8.4 %collective-permute-start.17 = (bf16[3,64,512]{2,1,0:T(8,128)(2,1)S(1)}, bf16[3,64,512]{2,1,0:T(8,128)(2,1)}, u32[]{:S(2)}, u32[]{:S(2)}) collective-permute-start(bf16[3,64,512]{2,1,0:T(8,128)(2,1)S(1)} %collective-permute-done.4.refs_10_), channel_id=1, source_target_pairs={{0,1},{1,0},{2,3},{3,2},{4,5},{5,4},{6,7},{7,6},{8,9},{9,8},{10,11... | collective-permute-start | bytes 589832 | tf_op jit(solution)/shard_map/ppermute | solution.py:26
  50.6 7.9 %collective-permute-start.16 = (bf16[3,64,512]{2,1,0:T(8,128)(2,1)}, bf16[3,64,512]{2,1,0:T(8,128)(2,1)}, u32[]{:S(2)}, u32[]{:S(2)}) collective-permute-start(bf16[3,64,512]{2,1,0:T(8,128)(2,1)} %collective-permute-done.6.refs_9_), channel_id=1, source_target_pairs={{0,1},{1,0},{2,3},{3,2},{4,5},{5,4},{6,7},{7,6},{8,9},{9,8},{10,11... | collective-permute-start | bytes 589832 | tf_op jit(solution)/shard_map/ppermute | solution.py:26
  50.8 7.8 %collective-permute-start.19 = (bf16[3,64,512]{2,1,0:T(8,128)(2,1)}, bf16[3,64,512]{2,1,0:T(8,128)(2,1)}, u32[]{:S(2)}, u32[]{:S(2)}) collective-permute-start(bf16[3,64,512]{2,1,0:T(8,128)(2,1)} %collective-permute-done.14.refs_15_), channel_id=1, source_target_pairs={{0,1},{1,0},{2,3},{3,2},{4,5},{5,4},{6,7},{7,6},{8,9},{9,8},{10,11... | collective-permute-start | bytes 589832 | tf_op jit(solution)/shard_map/ppermute | solution.py:26
  57.9 1.8 collective-permute-start.15
  66.1 16.5 %collective-permute-start.22 = (f32[4,96,768]{2,1,0:T(8,128)}, f32[4,96,768]{2,1,0:T(8,128)S(1)}, u32[]{:S(2)}, u32[]{:S(2)}) collective-permute-start(f32[4,96,768]{2,1,0:T(8,128)} %get-tuple-element.56), channel_id=1, source_target_pairs={{0,6},{1,25},{2,0},{3,27},{4,2},{5,29},{6,4},{7,31},{8,14},{9,1},{... | collective-permute-start | bytes 3538952 | tf_op jit(solution)/shard_map/ppermute | solution.py:26
  66.3 19.3 %collective-permute-start.25 = (f32[4,96,768]{2,1,0:T(8,128)}, f32[4,96,768]{2,1,0:T(8,128)S(1)}, u32[]{:S(2)}, u32[]{:S(2)}) collective-permute-start(f32[4,96,768]{2,1,0:T(8,128)} %get-tuple-element.71), channel_id=1, source_target_pairs={{0,2},{1,9},{2,4},{3,11},{4,6},{5,13},{6,0},{7,15},{8,10},{9,17},{... | collective-permute-start | bytes 3538952 | tf_op jit(solution)/shard_map/ppermute | solution.py:26
  78.2 20.5 %collective-permute-start.21 = (f32[4,96,768]{2,1,0:T(8,128)}, f32[4,96,768]{2,1,0:T(8,128)}, u32[]{:S(2)}, u32[]{:S(2)}) collective-permute-start(f32[4,96,768]{2,1,0:T(8,128)} %get-tuple-element.67), channel_id=1, source_target_pairs={{0,2},{1,9},{2,4},{3,11},{4,6},{5,13},{6,0},{7,15},{8,10},{9,17},{... | collective-permute-start | bytes 3538952 | tf_op jit(solution)/shard_map/ppermute | solution.py:26
  84.1 16.4 %collective-permute-start.23 = (f32[4,96,768]{2,1,0:T(8,128)S(1)}, f32[4,96,768]{2,1,0:T(8,128)}, u32[]{:S(2)}, u32[]{:S(2)}) collective-permute-start(f32[4,96,768]{2,1,0:T(8,128)S(1)} %add.158), channel_id=1, source_target_pairs={{0,6},{1,25},{2,0},{3,27},{4,2},{5,29},{6,4},{7,31},{8,14},{9,1},{... | collective-permute-start | bytes 3538952 | tf_op jit(solution)/shard_map/ppermute | solution.py:26
  85.5 27.6 %collective-permute-start.24 = (f32[4,96,768]{2,1,0:T(8,128)}, f32[4,96,768]{2,1,0:T(8,128)}, u32[]{:S(2)}, u32[]{:S(2)}) collective-permute-start(f32[4,96,768]{2,1,0:T(8,128)} %get-tuple-element.69), channel_id=1, source_target_pairs={{0,6},{1,25},{2,0},{3,27},{4,2},{5,29},{6,4},{7,31},{8,14},{9,1},{... | collective-permute-start | bytes 3538952 | tf_op jit(solution)/shard_map/ppermute | solution.py:26
  85.8 27.3 %collective-permute-start.26 = (f32[4,96,768]{2,1,0:T(8,128)S(1)}, f32[4,96,768]{2,1,0:T(8,128)S(1)}, u32[]{:S(2)}, u32[]{:S(2)}) collective-permute-start(f32[4,96,768]{2,1,0:T(8,128)S(1)} %add.162), channel_id=1, source_target_pairs={{0,2},{1,9},{2,4},{3,11},{4,6},{5,13},{6,0},{7,15},{8,10},{9,17},{... | collective-permute-start | bytes 3538952 | tf_op jit(solution)/shard_map/ppermute | solution.py:26
  96.1 2.6 %collective-permute-start.20 = (bf16[4,3,64,512]{3,2,1,0:T(8,128)(2,1)}, bf16[4,3,64,512]{3,2,1,0:T(8,128)(2,1)}, u32[]{:S(2)}, u32[]{:S(2)}) collective-permute-start(bf16[4,3,64,512]{3,2,1,0:T(8,128)(2,1)} %shard_map.79.refs_4_), channel_id=1, source_target_pairs={{0,1},{1,0},{2,3},{3,2},{4,5},{5,4},{6,7},{7,6},{8,9},{9,8},{10,11... | collective-permute-start | bytes 2359304 | tf_op jit(solution)/shard_map/ppermute | solution.py:26
  100.5 16.9 %copy-start.11 = (f32[4,96,768]{2,1,0:T(8,128)S(1)}, f32[4,96,768]{2,1,0:T(8,128)}, u32[]{:S(2)}) copy-start(f32[4,96,768]{2,1,0:T(8,128)} %get-tuple-element.60) | copy-start | bytes 3538948
  115.0 8.1 %collective-permute-start.28 = (f32[96,768]{1,0:T(8,128)}, f32[96,768]{1,0:T(8,128)}, u32[]{:S(2)}, u32[]{:S(2)}) collective-permute-start(f32[96,768]{1,0:T(8,128)} %add_bitcast_fusion.5), channel_id=1, source_target_pairs={{0,24},{1,7},{2,26},{3,1},{4,28},{5,3},{6,30},{7,5},{8,0},{9,15},{... | collective-permute-start | bytes 884744 | tf_op jit(solution)/shard_map/ppermute | solution.py:26
  117.4 10.9 %collective-permute-start.31 = (f32[96,768]{1,0:T(8,128)}, f32[96,768]{1,0:T(8,128)}, u32[]{:S(2)}, u32[]{:S(2)}) collective-permute-start(f32[96,768]{1,0:T(8,128)} %add_bitcast_fusion.4), channel_id=1, source_target_pairs={{0,8},{1,3},{2,10},{3,5},{4,12},{5,7},{6,14},{7,1},{8,16},{9,11},{... | collective-permute-start | bytes 884744 | tf_op jit(solution)/shard_map/ppermute | solution.py:26
  120.9 11.2 %collective-permute-start.27 = (f32[96,768]{1,0:T(8,128)}, f32[96,768]{1,0:T(8,128)}, u32[]{:S(2)}, u32[]{:S(2)}) collective-permute-start(f32[96,768]{1,0:T(8,128)} %add_bitcast_fusion.3), channel_id=1, source_target_pairs={{0,8},{1,3},{2,10},{3,5},{4,12},{5,7},{6,14},{7,1},{8,16},{9,11},{... | collective-permute-start | bytes 884744 | tf_op jit(solution)/shard_map/ppermute | solution.py:26
  122.8 9.3 %collective-permute-start.30 = (f32[96,768]{1,0:T(8,128)}, f32[96,768]{1,0:T(8,128)}, u32[]{:S(2)}, u32[]{:S(2)}) collective-permute-start(f32[96,768]{1,0:T(8,128)} %add_bitcast_fusion.2), channel_id=1, source_target_pairs={{0,24},{1,7},{2,26},{3,1},{4,28},{5,3},{6,30},{7,5},{8,0},{9,15},{... | collective-permute-start | bytes 884744 | tf_op jit(solution)/shard_map/ppermute | solution.py:26
  125.0 8.9 %collective-permute-start.29 = (f32[96,768]{1,0:T(8,128)}, f32[96,768]{1,0:T(8,128)}, u32[]{:S(2)}, u32[]{:S(2)}) collective-permute-start(f32[96,768]{1,0:T(8,128)} %bitcast_add_fusion.1), channel_id=1, source_target_pairs={{0,24},{1,7},{2,26},{3,1},{4,28},{5,3},{6,30},{7,5},{8,0},{9,15},{... | collective-permute-start | bytes 884744 | tf_op jit(solution)/shard_map/ppermute | solution.py:26
  130.1 7.0 %collective-permute-start.32 = (f32[96,768]{1,0:T(8,128)}, f32[96,768]{1,0:T(8,128)}, u32[]{:S(2)}, u32[]{:S(2)}) collective-permute-start(f32[96,768]{1,0:T(8,128)} %bitcast_add_fusion), channel_id=1, source_target_pairs={{0,8},{1,3},{2,10},{3,5},{4,12},{5,7},{6,14},{7,1},{8,16},{9,11},{... | collective-permute-start | bytes 884744 | tf_op jit(solution)/shard_map/ppermute | solution.py:26
  140.4 7.0 %collective-permute-start.33 = (f32[3,96,128]{2,1,0:T(8,128)}, f32[3,96,128]{2,1,0:T(8,128)S(1)}, u32[]{:S(2)}, u32[]{:S(2)}) collective-permute-start(f32[3,96,128]{2,1,0:T(8,128)} %get-tuple-element.80), channel_id=1, source_target_pairs={{0,2},{1,3},{2,4},{3,5},{4,6},{5,7},{6,0},{7,1},{8,10},{9,11},{10,... | collective-permute-start | bytes 442376 | tf_op jit(solution)/shard_map/ppermute | solution.py:26
  142.3 8.2 %collective-permute-start.34 = (f32[3,96,128]{2,1,0:T(8,128)}, f32[3,96,128]{2,1,0:T(8,128)S(1)}, u32[]{:S(2)}, u32[]{:S(2)}) collective-permute-start(f32[3,96,128]{2,1,0:T(8,128)} %get-tuple-element.81), channel_id=1, source_target_pairs={{0,4},{1,5},{2,6},{3,7},{4,0},{5,1},{6,2},{7,3},{8,12},{9,13},{10,... | collective-permute-start | bytes 442376 | tf_op jit(solution)/shard_map/ppermute | solution.py:26
  145.5 5.4 %collective-permute-start.35 = (f32[3,96,128]{2,1,0:T(8,128)}, f32[3,96,128]{2,1,0:T(8,128)S(1)}, u32[]{:S(2)}, u32[]{:S(2)}) collective-permute-start(f32[3,96,128]{2,1,0:T(8,128)} %get-tuple-element.82), channel_id=1, source_target_pairs={{0,6},{1,7},{2,0},{3,1},{4,2},{5,3},{6,4},{7,5},{8,14},{9,15},{10,... | collective-permute-start | bytes 442376 | tf_op jit(solution)/shard_map/ppermute | solution.py:26
  155.5 2.3 collective-permute-start.36
  237.5 5.0 %collective-permute-start.37 = (f32[16,8,5,8,128]{4,3,2,1,0:T(8,128)S(1)}, f32[16,8,5,8,128]{4,3,2,1,0:T(8,128)}, u32[]{:S(2)}, u32[]{:S(2)}) collective-permute-start(f32[16,8,5,8,128]{4,3,2,1,0:T(8,128)S(1)} %all_to_all.23.plane), channel_id=1, source_target_pairs={{0,1},{1,0},{2,3},{3,2},{4,5},{5,4},{6,7},{7,6},{8,9},{9,8},{10,11... | collective-permute-start | bytes 7864328 | tf_op jit(solution)/shard_map/ppermute | solution.py:26
  (8 other events, 29.8 us)
where the time goes:
time: 255 us; the launch traced here: 251 us
  blocking collectives  78.2 us (31%)
  waiting for transfers between devices  69.9 us (27%)
  starting transfers between devices  40.8 us (16%)
  Pallas kernels  40.5 us (16%)
  other arithmetic  16.8 us (7%)
  local copies, waits for them, and re-layouts  4.21 us (2%)
    ppermute x37, waiting for transfers between devices, hop(): return lax.ppermute(value, AXES, pairs)  58.9 us
    ppermute x37, starting transfers between devices, hop(): return lax.ppermute(value, AXES, pairs)  38.9 us
    all_to_all x1, blocking collectives, on_device(): lax.all_to_all(jnp.broadcast_to(over_z, (16,) + over_z.shape), ('y', 'x')...  34.5 us
    pallas_call x3, Pallas kernels, products(): pl.pallas_call(kernel, grid_spec=pltpu.PrefetchScalarGridSpec(num_scalar_...  22.5 us
    all_to_all x1, blocking collectives, on_device(): sums = jnp.sum(lax.all_to_all(sums, 'z', 0, 0, tiled=True), axis=0)  16.2 us
    all_to_all x1, blocking collectives, on_device(): lax.all_to_all(keep + swap_cores(send), 'y', 0, 0, tiled=True)  15.6 us
    all_to_all x1, blocking collectives, on_device(): lax.all_to_all(jnp.broadcast_to(sums, (8,) + sums.shape), 'z', 0, 0, tile...  11.8 us
    ppermute x1, waiting for transfers between devices, to_column(): return lax.ppermute(value, AXES, pairs)  11 us
  transfers between devices with their start and end apart: 38, of which 18 were waited for; matrix products, arithmetic and copies ran while one was open for 7% of the time, Pallas kernels for 7%

commit v1 on v0

--- a/solution.py
+++ b/solution.py
@@ -422,6 +422,8 @@
     near = stacked(near)
     near_other = swap_cores(near)
     low, high = ring_sum(own, raw[0:2], middle, raw[2:4], step_first)
+    low = (lax.optimization_barrier(low[0] + low[1]), low[2])
+    high = (lax.optimization_barrier(high[0] + high[1]), high[2])
     here, near, near_other = lax.optimization_barrier((jnp.where(k == 0, y, x), near, near_other))
 
     def regroup(offset, here):
@@ -437,7 +439,9 @@
     low, high = ring_sum(own_share, behind_share, far, ahead_share, step_second)
     panels, spread = chain(place, [(low, high)], parent_factor, node_count)
 
-    block_panels = [spread[0]] + [step_x(spread[d], d) for d in range(1, 4)]
+    block_panels = [spread[0]]
+    for d in range(1, 4):
+        block_panels.append(step_x(spread[d], d))
     keep, send = contraction(place, slot_tiles, block_panels, near, near_other)
     sums = jnp.sum(lax.all_to_all(keep + swap_cores(send), "y", 0, 0, tiled=True), axis=0)
     sums = jnp.sum(lax.all_to_all(sums, "z", 0, 0, tiled=True), axis=0)

time: 255 us -> 252 us (0.988)
  waiting for transfers between devices: 69.9 us -> 58.8 us
  blocking collectives: 78.2 us -> 80.8 us
    ppermute x37, waiting for transfers between devices: 58.9 us -> 47.8 us  [hop(): return lax.ppermute(value, AXES, pairs)]
    add x2, other arithmetic: 1.98 us -> 4.7 us  [ring_sum(): joined_high = ahead[1] + far_high]
  transfers between devices with their start and end apart: 38 -> 38, of which waited for: 18 -> 17; matrix products, arithmetic and copies ran while one was open for 7% -> 8% of each run, Pallas kernels for 7% -> 7%
where the time goes in v1:
time: 252 us; the launch traced here: 248 us
  blocking collectives  80.8 us (32%)
  waiting for transfers between devices  58.8 us (23%)
  starting transfers between devices  42.4 us (17%)
  Pallas kernels  40.5 us (16%)
  other arithmetic  18.5 us (7%)
  local copies, waits for them, and re-layouts  5.88 us (2%)
    ppermute x37, waiting for transfers between devices, hop(): return lax.ppermute(value, AXES, pairs)  47.8 us
    ppermute x37, starting transfers between devices, hop(): return lax.ppermute(value, AXES, pairs)  40.4 us
    all_to_all x1, blocking collectives, on_device(): lax.all_to_all(jnp.broadcast_to(over_z, (16,) + over_z.shape), ('y', 'x')...  34.7 us
    pallas_call x3, Pallas kernels, products(): pl.pallas_call(kernel, grid_spec=pltpu.PrefetchScalarGridSpec(num_scalar_...  22.5 us
    all_to_all x1, blocking collectives, on_device(): sums = jnp.sum(lax.all_to_all(sums, 'z', 0, 0, tiled=True), axis=0)  18.7 us
    all_to_all x1, blocking collectives, on_device(): lax.all_to_all(keep + swap_cores(send), 'y', 0, 0, tiled=True)  15.6 us
    all_to_all x1, blocking collectives, on_device(): lax.all_to_all(jnp.broadcast_to(sums, (8,) + sums.shape), 'z', 0, 0, tile...  11.8 us
    ppermute x1, waiting for transfers between devices, to_column(): return lax.ppermute(value, AXES, pairs)  11 us
  transfers between devices with their start and end apart: 38, of which 17 were waited for; matrix products, arithmetic and copies ran while one was open for 8% of the time, Pallas kernels for 7%

profile of v1, /device:TPU:8, one launch (start us, length us, event | category | flops | bytes accessed | tf_op | source)
XLA Modules:
  0.0 247.8 jit_solution(13361555327156490143)
XLA Ops:
  0.6 2.8 %collective-permute-start.1 = (bf16[3,64,512]{2,1,0:T(8,128)(2,1)}, bf16[3,64,512]{2,1,0:T(8,128)(2,1)S(1)}, u32[]{:S(2)}, u32[]{:S(2)}) collective-permute-start(bf16[3,64,512]{2,1,0:T(8,128)(2,1)} %refs_0_), channel_id=1, source_target_pairs={{0,6},{1,7},{2,0},{3,1},{4,2},{5,3},{6,4},{7,5},{8,14},{9,15},{10,... | collective-permute-start | bytes 589832 | tf_op jit(solution)/shard_map/ppermute | solution.py:26
  3.5 1.9 collective-permute-start
  5.4 3.8 %collective-permute-start.2 = (bf16[3,64,512]{2,1,0:T(8,128)(2,1)}, bf16[3,64,512]{2,1,0:T(8,128)(2,1)}, u32[]{:S(2)}, u32[]{:S(2)}) collective-permute-start(bf16[3,64,512]{2,1,0:T(8,128)(2,1)} %refs_0_), channel_id=1, source_target_pairs={{0,2},{1,3},{2,4},{3,5},{4,6},{5,7},{6,0},{7,1},{8,10},{9,11},{10,... | collective-permute-start | bytes 589832 | tf_op jit(solution)/shard_map/ppermute | solution.py:26
  9.2 3.2 %dynamic-slice_bitcast_fusion = bf16[4,4,96,768]{3,2,1,0:T(8,128)(2,1)} fusion(bf16[4,4,2,96,768]{4,3,2,1,0:T(8,128)(2,1)} %bitcast.23, s32[]{:T(128)S(6)} %select_n.59), kind=kLoop, calls=%fused_computation | loop fusion | bytes 4718596 | tf_op jit(solution)/shard_map/jit(dynamic_index_in_dim)/squeeze | solution.py:60
  12.5 11.0 %collective-permute-done.refs_12_ = bf16[3,64,512]{2,1,0:T(8,128)(2,1)S(1)} collective-permute-done((bf16[3,64,512]{2,1,0:T(8,128)(2,1)}, bf16[3,64,512]{2,1,0:T(8,128)(2,1)S(1)}, u32[]{:S(2)}, u32[]{:S(2)}) %collective-permute-start) | collective-permute-done | bytes 196640 | tf_op jit(solution)/shard_map/ppermute | solution.py:52
  24.0 3.7 %collective-permute-start.8 = (bf16[3,64,512]{2,1,0:T(8,128)(2,1)S(1)}, bf16[3,64,512]{2,1,0:T(8,128)(2,1)S(1)}, u32[]{:S(2)}, u32[]{:S(2)}) collective-permute-start(bf16[3,64,512]{2,1,0:T(8,128)(2,1)S(1)} %collective-permute-done.refs_12_), channel_id=1, source_target_pairs={{0,224},{1,225},{2,226},{3,227},{4,228},{5,229},{6,230},{7,231},{8... | collective-permute-start | bytes 589832 | tf_op jit(solution)/shard_map/ppermute | solution.py:26
  27.9 5.3 %collective-permute-done.3.refs_11_ = bf16[3,64,512]{2,1,0:T(8,128)(2,1)S(1)} collective-permute-done((bf16[3,64,512]{2,1,0:T(8,128)(2,1)S(1)}, bf16[3,64,512]{2,1,0:T(8,128)(2,1)S(1)}, u32[]{:S(2)}, u32[]{:S(2)}) %collective-permute-start.3) | collective-permute-done | bytes 196640 | tf_op jit(solution)/shard_map/ppermute | solution.py:26
  34.1 3.3 %collective-permute-start.13 = (bf16[3,64,512]{2,1,0:T(8,128)(2,1)S(1)}, bf16[3,64,512]{2,1,0:T(8,128)(2,1)S(1)}, u32[]{:S(2)}, u32[]{:S(2)}) collective-permute-start(bf16[3,64,512]{2,1,0:T(8,128)(2,1)S(1)} %collective-permute-done.8.refs_13_), channel_id=1, source_target_pairs={{0,224},{1,225},{2,226},{3,227},{4,228},{5,229},{6,230},{7,231},{8... | collective-permute-start | bytes 589832 | tf_op jit(solution)/shard_map/ppermute | solution.py:26
  37.4 4.0 %collective-permute-done.4.refs_10_ = bf16[3,64,512]{2,1,0:T(8,128)(2,1)S(1)} collective-permute-done((bf16[3,64,512]{2,1,0:T(8,128)(2,1)S(1)}, bf16[3,64,512]{2,1,0:T(8,128)(2,1)S(1)}, u32[]{:S(2)}, u32[]{:S(2)}) %collective-permute-start.4) | collective-permute-done | bytes 196640 | tf_op jit(solution)/shard_map/ppermute | solution.py:26
  41.9 3.7 %collective-permute-start.14 = (bf16[3,64,512]{2,1,0:T(8,128)(2,1)S(1)}, bf16[3,64,512]{2,1,0:T(8,128)(2,1)}, u32[]{:S(2)}, u32[]{:S(2)}) collective-permute-start(bf16[3,64,512]{2,1,0:T(8,128)(2,1)S(1)} %collective-permute-done.13.refs_14_), channel_id=1, source_target_pairs={{0,224},{1,225},{2,226},{3,227},{4,228},{5,229},{6,230},{7,231},{8... | collective-permute-start | bytes 589832 | tf_op jit(solution)/shard_map/ppermute | solution.py:26
  45.6 4.4 %collective-permute-done.6.refs_9_ = bf16[3,64,512]{2,1,0:T(8,128)(2,1)} collective-permute-done((bf16[3,64,512]{2,1,0:T(8,128)(2,1)S(1)}, bf16[3,64,512]{2,1,0:T(8,128)(2,1)}, u32[]{:S(2)}, u32[]{:S(2)}) %collective-permute-start.6) | collective-permute-done | bytes 196640 | tf_op jit(solution)/shard_map/ppermute | solution.py:26
  51.2 6.8 %collective-permute-done.12.refs_8_ = bf16[3,64,512]{2,1,0:T(8,128)(2,1)} collective-permute-done((bf16[3,64,512]{2,1,0:T(8,128)(2,1)}, bf16[3,64,512]{2,1,0:T(8,128)(2,1)}, u32[]{:S(2)}, u32[]{:S(2)}) %collective-permute-start.12) | collective-permute-done | bytes 196640 | tf_op jit(solution)/shard_map/ppermute | solution.py:26
  58.6 1.2 collective-permute-done.15.refs_16_
  59.8 6.2 %shard_map.76 = (f32[4,96,768]{2,1,0:T(8,128)}, f32[4,96,768]{2,1,0:T(8,128)}) custom-call(s32[4]{0:T(128)} %pad_add_fusion.place, s32[3,64]{1,0:T(4,128)} %tiles.7, bf16[4,4,2,96,768]{4,3,2,1,0:T(8,128)(2,1)} %bitcast.24, bf16[4,4,2,96,768]{4,3,2,1,0:T(8,128)(2,1)} %bitcast.25, bf16[4,4,2,96,768]{4,3,2,1,0:T(8,128)(2,1)} %bitcast.26, ...), custom_call_target="tpu_custom_call" | custom-call | tf_op jit(solution)/shard_map/pallas_call | solution.py:168
  66.2 3.1 %collective-permute-start.22 = (f32[4,96,768]{2,1,0:T(8,128)}, f32[4,96,768]{2,1,0:T(8,128)S(1)}, u32[]{:S(2)}, u32[]{:S(2)}) collective-permute-start(f32[4,96,768]{2,1,0:T(8,128)} %get-tuple-element.56), channel_id=1, source_target_pairs={{0,6},{1,25},{2,0},{3,27},{4,2},{5,29},{6,4},{7,31},{8,14},{9,1},{... | collective-permute-start | bytes 3538952 | tf_op jit(solution)/shard_map/ppermute | solution.py:26
  69.3 10.0 %shard_map.77 = (f32[4,96,768]{2,1,0:T(8,128)}, f32[4,96,768]{2,1,0:T(8,128)}, f32[4,96,768]{2,1,0:T(8,128)}, f32[4,96,768]{2,1,0:T(8,128)}) custom-call(s32[4]{0:T(128)} %pad_add_fusion.place, s32[3,64]{1,0:T(4,128)} %tiles.7, bf16[4,4,2,96,768]{4,3,2,1,0:T(8,128)(2,1)} %bitcast.28, bf16[4,4,2,96,768]{4,3,2,1,0:T(8,128)(2,1)} %bitcast.29, ...), custom_call_target="tpu_custom_call" | custom-call | tf_op jit(solution)/shard_map/pallas_call | solution.py:168
  79.5 3.2 %collective-permute-start.24 = (f32[4,96,768]{2,1,0:T(8,128)}, f32[4,96,768]{2,1,0:T(8,128)S(1)}, u32[]{:S(2)}, u32[]{:S(2)}) collective-permute-start(f32[4,96,768]{2,1,0:T(8,128)} %get-tuple-element.69), channel_id=1, source_target_pairs={{0,6},{1,25},{2,0},{3,27},{4,2},{5,29},{6,4},{7,31},{8,14},{9,1},{... | collective-permute-start | bytes 3538952 | tf_op jit(solution)/shard_map/ppermute | solution.py:26
  82.7 1.1 collective-permute-done.25
  83.8 2.9 %add.128 = f32[4,96,768]{2,1,0:T(8,128)} add(f32[4,96,768]{2,1,0:T(8,128)} %get-tuple-element.70, f32[4,96,768]{2,1,0:T(8,128)} %collective-permute-done.25) | non-fusion elementwise | flops 294912 | bytes 3538944 | tf_op jit(solution)/shard_map/add | solution.py:361
  86.7 1.2 add.124
  87.9 3.2 %collective-permute-start.23 = (f32[4,96,768]{2,1,0:T(8,128)}, f32[4,96,768]{2,1,0:T(8,128)}, u32[]{:S(2)}, u32[]{:S(2)}) collective-permute-start(f32[4,96,768]{2,1,0:T(8,128)} %add.124), channel_id=1, source_target_pairs={{0,6},{1,25},{2,0},{3,27},{4,2},{5,29},{6,4},{7,31},{8,14},{9,1},{... | collective-permute-start | bytes 3538952 | tf_op jit(solution)/shard_map/ppermute | solution.py:26
  91.1 6.2 %shard_map.78 = (f32[4,96,768]{2,1,0:T(8,128)}, f32[4,96,768]{2,1,0:T(8,128)}) custom-call(s32[4]{0:T(128)} %pad_add_fusion.place, s32[3,64]{1,0:T(4,128)} %tiles.7, bf16[4,4,2,96,768]{4,3,2,1,0:T(8,128)(2,1)} %bitcast.32, bf16[4,4,2,96,768]{4,3,2,1,0:T(8,128)(2,1)} %bitcast.33, bf16[4,4,2,96,768]{4,3,2,1,0:T(8,128)(2,1)} %bitcast.34, ...), custom_call_target="tpu_custom_call" | custom-call | tf_op jit(solution)/shard_map/pallas_call | solution.py:168
  97.4 2.2 shard_map.79.refs_4_
  99.5 2.5 %collective-permute-done.21.refs_5_ = bf16[4,3,64,512]{3,2,1,0:T(8,128)(2,1)S(1)} collective-permute-done((bf16[4,3,64,512]{3,2,1,0:T(8,128)(2,1)}, bf16[4,3,64,512]{3,2,1,0:T(8,128)(2,1)S(1)}, u32[]{:S(2)}, u32[]{:S(2)}) %collective-permute-start.21) | collective-permute-done | bytes 786464 | tf_op jit(solution)/shard_map/ppermute | solution.py:26
  102.9 1.5 add.120
  104.7 5.1 %collective-permute-done.26 = f32[4,96,768]{2,1,0:T(8,128)} collective-permute-done((f32[4,96,768]{2,1,0:T(8,128)}, f32[4,96,768]{2,1,0:T(8,128)}, u32[]{:S(2)}, u32[]{:S(2)}) %collective-permute-start.26) | collective-permute-done | bytes 1179680 | tf_op jit(solution)/shard_map/ppermute | solution.py:26
  111.8 2.3 collective-permute-start.28
  114.2 1.9 add_bitcast_fusion.2
  116.2 1.9 collective-permute-start.27
  118.9 1.8 bitcast_add_fusion.1
  120.8 2.3 collective-permute-start.29
  123.1 1.8 bitcast_add_fusion
  124.9 1.7 add_bitcast_fusion.1.refs_0_
  126.6 1.7 add_bitcast_fusion.refs_3_
  128.3 3.5 %collective-permute-done.32.refs_5_ = f32[96,768]{1,0:T(8,128)S(1)} collective-permute-done((f32[96,768]{1,0:T(8,128)}, f32[96,768]{1,0:T(8,128)S(1)}, u32[]{:S(2)}, u32[]{:S(2)}) %collective-permute-start.32) | collective-permute-done | bytes 294944 | tf_op jit(solution)/shard_map/ppermute | solution.py:26
  132.5 3.2 %chain.1 = (bf16[3,96,512]{2,1,0:T(8,128)(2,1)}, f32[3,96,128]{2,1,0:T(8,128)}, f32[3,96,128]{2,1,0:T(8,128)}, f32[3,96,128]{2,1,0:T(8,128)}, f32[3,96,128]{2,1,0:T(8,128)}) custom-call(s32[4]{0:T(128)} %pad_add_fusion.place, f32[96,768]{1,0:T(8,128)} %add_bitcast_fusion.1.refs_0_, f32[96,768]{1,0:T(8,128)} %copy-done.14, f32[96,768]{1,0:T(8,128)} %copy-done.16, ...), custom_call_target="tpu_custom_call" | custom-call | tf_op jit(solution)/shard_map/chain/pallas_call | solution.py:226
  136.1 3.4 %collective-permute-start.34 = (f32[3,96,128]{2,1,0:T(8,128)}, f32[3,96,128]{2,1,0:T(8,128)S(1)}, u32[]{:S(2)}, u32[]{:S(2)}) collective-permute-start(f32[3,96,128]{2,1,0:T(8,128)} %get-tuple-element.81), channel_id=1, source_target_pairs={{0,4},{1,5},{2,6},{3,7},{4,0},{5,1},{6,2},{7,3},{8,12},{9,13},{10,... | collective-permute-start | bytes 442376 | tf_op jit(solution)/shard_map/ppermute | solution.py:26
  139.5 2.9 %collective-permute-done.33.refs_1_ = f32[3,96,128]{2,1,0:T(8,128)S(1)} collective-permute-done((f32[3,96,128]{2,1,0:T(8,128)}, f32[3,96,128]{2,1,0:T(8,128)S(1)}, u32[]{:S(2)}, u32[]{:S(2)}) %collective-permute-start.33) | collective-permute-done | bytes 147488 | tf_op jit(solution)/shard_map/ppermute | solution.py:26
  142.4 2.0 collective-permute-done.34.refs_2_
  145.5 3.9 %contraction.1 = (f32[4,8,5,8,128]{4,3,2,1,0:T(8,128)}, f32[4,8,5,8,128]{4,3,2,1,0:T(8,128)}) custom-call(s32[4]{0:T(128)} %pad_add_fusion.place, s32[3,64]{1,0:T(4,128)} %tiles.7, f32[3,96,128]{2,1,0:T(8,128)} %get-tuple-element.79.refs_0_, f32[3,96,128]{2,1,0:T(8,128)} %copy-done.19, f32[3,96,128]{2,1,0:T(8,128)} %copy-done.20, f32[3,96,128]{2,1,0:T(8,128)} %copy-done.21, ...), custom_call_target="tpu_custom_call" | custom-call | tf_op jit(solution)/shard_map/contraction/pallas_call | solution.py:300
  149.4 2.3 collective-permute-done.36
  151.7 1.2 add.153
  152.9 15.6 %all_to_all.20 = f32[4,8,5,8,128]{4,3,2,1,0:T(8,128)S(1)} all-to-all(f32[4,8,5,8,128]{4,3,2,1,0:T(8,128)S(1)} %add.153), channel_id=1, replica_groups=mesh['z'=8,'y'=4,'x'=4,'k'=2] {'y'}, dimensions={0} | all-to-all | bytes 1310720 | tf_op jit(solution)/shard_map/all_to_all | solution.py:446
  168.5 18.7 %all_to_all.21 = f32[8,5,8,128]{3,2,1,0:T(8,128)S(1)} all-to-all(f32[8,5,8,128]{3,2,1,0:T(8,128)S(1)} %reduce_sum.18), channel_id=1, replica_groups=mesh['z'=8,'y'=4,'x'=4,'k'=2] {'z'}, dimensions={0} | all-to-all | bytes 327680 | tf_op jit(solution)/shard_map/all_to_all | solution.py:447
  187.2 11.8 %all_to_all.22 = f32[8,5,8,128]{3,2,1,0:T(8,128)S(1)} all-to-all(f32[8,5,8,128]{3,2,1,0:T(8,128)S(1)} %broadcast_in_dim.6), channel_id=1, replica_groups=mesh['z'=8,'y'=4,'x'=4,'k'=2] {'z'}, dimensions={0} | all-to-all | bytes 327680 | tf_op jit(solution)/shard_map/all_to_all | solution.py:448
  199.3 34.7 %all_to_all.23.plane = f32[16,8,5,8,128]{4,3,2,1,0:T(8,128)S(1)} all-to-all(f32[16,8,5,8,128]{4,3,2,1,0:T(8,128)S(1)} %broadcast_in_dim.7), channel_id=1, replica_groups=mesh['z'=8,'y'=4,'x'=4,'k'=2] {'y','x'}, dimensions={0} | all-to-all | bytes 5242880 | tf_op jit(solution)/shard_map/all_to_all | solution.py:449
  234.0 5.0 %collective-permute-done.37.other = f32[16,8,5,8,128]{4,3,2,1,0:T(8,128)} collective-permute-done((f32[16,8,5,8,128]{4,3,2,1,0:T(8,128)S(1)}, f32[16,8,5,8,128]{4,3,2,1,0:T(8,128)}, u32[]{:S(2)}, u32[]{:S(2)}) %collective-permute-start.37) | collective-permute-done | bytes 2621472 | tf_op jit(solution)/shard_map/ppermute | solution.py:26
  239.1 8.7 %tail.1 = (f32[3,512,512]{2,1,0:T(8,128)}, f32[2,512,512]{2,1,0:T(8,128)}) custom-call(s32[4]{0:T(128)} %pad_add_fusion.place, f32[16,8,5,8,128]{4,3,2,1,0:T(8,128)} %copy-done.1, f32[16,8,5,8,128]{4,3,2,1,0:T(8,128)} %collective-permute-done.37.other, bf16[2,512,512]{2,1,0:T(8,128)(2,1)} %links.1, f32[3,512,512]{2,1,0:T(8,128)} %diag_inverse.1), custom_call_target="tpu_custom_call" | custom-call | tf_op jit(solution)/shard_map/tail/pallas_call | solution.py:342
  (102 shorter events, 10.7 us)
Async XLA Ops:
  0.6 11.8 %collective-permute-start.1 = (bf16[3,64,512]{2,1,0:T(8,128)(2,1)}, bf16[3,64,512]{2,1,0:T(8,128)(2,1)S(1)}, u32[]{:S(2)}, u32[]{:S(2)}) collective-permute-start(bf16[3,64,512]{2,1,0:T(8,128)(2,1)} %refs_0_), channel_id=1, source_target_pairs={{0,6},{1,7},{2,0},{3,1},{4,2},{5,3},{6,4},{7,5},{8,14},{9,15},{10,... | collective-permute-start | bytes 589832 | tf_op jit(solution)/shard_map/ppermute | solution.py:26
  3.5 20.0 %collective-permute-start = (bf16[3,64,512]{2,1,0:T(8,128)(2,1)}, bf16[3,64,512]{2,1,0:T(8,128)(2,1)S(1)}, u32[]{:S(2)}, u32[]{:S(2)}) collective-permute-start(bf16[3,64,512]{2,1,0:T(8,128)(2,1)} %refs_0_), channel_id=1, source_target_pairs={{0,0},{1,32},{2,64},{3,96},{4,128},{5,160},{6,192},{7,224},{8,1},{... | collective-permute-start | bytes 589832 | tf_op jit(solution)/shard_map/ppermute | solution.py:52
  5.4 18.1 %collective-permute-start.2 = (bf16[3,64,512]{2,1,0:T(8,128)(2,1)}, bf16[3,64,512]{2,1,0:T(8,128)(2,1)}, u32[]{:S(2)}, u32[]{:S(2)}) collective-permute-start(bf16[3,64,512]{2,1,0:T(8,128)(2,1)} %refs_0_), channel_id=1, source_target_pairs={{0,2},{1,3},{2,4},{3,5},{4,6},{5,7},{6,0},{7,1},{8,10},{9,11},{10,... | collective-permute-start | bytes 589832 | tf_op jit(solution)/shard_map/ppermute | solution.py:26
  12.5 21.6 %copy-start.12 = (bf16[3,64,512]{2,1,0:T(8,128)(2,1)}, bf16[3,64,512]{2,1,0:T(8,128)(2,1)S(1)}, u32[]{:S(2)}) copy-start(bf16[3,64,512]{2,1,0:T(8,128)(2,1)S(1)} %collective-permute-done.1.refs_1_) | copy-start | bytes 589828
  23.4 36.3 %copy-start.2 = (bf16[3,64,512]{2,1,0:T(8,128)(2,1)}, bf16[3,64,512]{2,1,0:T(8,128)(2,1)S(1)}, u32[]{:S(2)}) copy-start(bf16[3,64,512]{2,1,0:T(8,128)(2,1)S(1)} %collective-permute-done.refs_12_) | copy-start | bytes 589828
  23.4 26.6 %collective-permute-start.10 = (bf16[4,4,96,768]{3,2,1,0:T(8,128)(2,1)}, bf16[4,4,96,768]{3,2,1,0:T(8,128)(2,1)S(1)}, u32[]{:S(2)}, u32[]{:S(2)}) collective-permute-start(bf16[4,4,96,768]{3,2,1,0:T(8,128)(2,1)} %dynamic-slice_bitcast_fusion), channel_id=1, source_target_pairs={{0,1},{1,0},{2,3},{3,2},{4,5},{5,4},{6,7},{7,6},{8,9},{9,8},{10,11... | collective-permute-start | bytes 7077896 | tf_op jit(solution)/shard_map/ppermute | solution.py:26
  23.5 9.8 %collective-permute-start.3 = (bf16[3,64,512]{2,1,0:T(8,128)(2,1)S(1)}, bf16[3,64,512]{2,1,0:T(8,128)(2,1)S(1)}, u32[]{:S(2)}, u32[]{:S(2)}) collective-permute-start(bf16[3,64,512]{2,1,0:T(8,128)(2,1)S(1)} %collective-permute-done.refs_12_), channel_id=1, source_target_pairs={{0,32},{1,33},{2,34},{3,35},{4,36},{5,37},{6,38},{7,39},{8,40},{9,... | collective-permute-start | bytes 589832 | tf_op jit(solution)/shard_map/ppermute | solution.py:26
  24.0 10.1 %collective-permute-start.8 = (bf16[3,64,512]{2,1,0:T(8,128)(2,1)S(1)}, bf16[3,64,512]{2,1,0:T(8,128)(2,1)S(1)}, u32[]{:S(2)}, u32[]{:S(2)}) collective-permute-start(bf16[3,64,512]{2,1,0:T(8,128)(2,1)S(1)} %collective-permute-done.refs_12_), channel_id=1, source_target_pairs={{0,224},{1,225},{2,226},{3,227},{4,228},{5,229},{6,230},{7,231},{8... | collective-permute-start | bytes 589832 | tf_op jit(solution)/shard_map/ppermute | solution.py:26
  27.6 9.7 %collective-permute-start.5 = (bf16[3,64,512]{2,1,0:T(8,128)(2,1)S(1)}, bf16[3,64,512]{2,1,0:T(8,128)(2,1)S(1)}, u32[]{:S(2)}, u32[]{:S(2)}) collective-permute-start(bf16[3,64,512]{2,1,0:T(8,128)(2,1)S(1)} %collective-permute-done.refs_12_), channel_id=1, source_target_pairs={{0,1},{1,0},{2,3},{3,2},{4,5},{5,4},{6,7},{7,6},{8,9},{9,8},{10,11... | collective-permute-start | bytes 589832 | tf_op jit(solution)/shard_map/ppermute | solution.py:26
  33.2 26.5 %copy-start.3 = (bf16[3,64,512]{2,1,0:T(8,128)(2,1)}, bf16[3,64,512]{2,1,0:T(8,128)(2,1)S(1)}, u32[]{:S(2)}) copy-start(bf16[3,64,512]{2,1,0:T(8,128)(2,1)S(1)} %collective-permute-done.3.refs_11_) | copy-start | bytes 589828
  33.2 8.2 %collective-permute-start.4 = (bf16[3,64,512]{2,1,0:T(8,128)(2,1)S(1)}, bf16[3,64,512]{2,1,0:T(8,128)(2,1)S(1)}, u32[]{:S(2)}, u32[]{:S(2)}) collective-permute-start(bf16[3,64,512]{2,1,0:T(8,128)(2,1)S(1)} %collective-permute-done.3.refs_11_), channel_id=1, source_target_pairs={{0,32},{1,33},{2,34},{3,35},{4,36},{5,37},{6,38},{7,39},{8,40},{9,... | collective-permute-start | bytes 589832 | tf_op jit(solution)/shard_map/ppermute | solution.py:26
  33.2 8.2 %collective-permute-start.11 = (bf16[3,64,512]{2,1,0:T(8,128)(2,1)S(1)}, bf16[3,64,512]{2,1,0:T(8,128)(2,1)S(1)}, u32[]{:S(2)}, u32[]{:S(2)}) collective-permute-start(bf16[3,64,512]{2,1,0:T(8,128)(2,1)S(1)} %broadcast_select_fusion), channel_id=1, source_target_pairs={{0,6},{1,3},{2,0},{3,5},{4,2},{5,7},{6,4},{7,1},{8,14},{9,11},{10,... | collective-permute-start | bytes 589832 | tf_op jit(solution)/shard_map/ppermute | solution.py:26
  34.1 25.7 %copy-start.4 = (bf16[3,64,512]{2,1,0:T(8,128)(2,1)}, bf16[3,64,512]{2,1,0:T(8,128)(2,1)S(1)}, u32[]{:S(2)}) copy-start(bf16[3,64,512]{2,1,0:T(8,128)(2,1)S(1)} %collective-permute-done.8.refs_13_) | copy-start | bytes 589828
  34.1 7.8 %collective-permute-start.13 = (bf16[3,64,512]{2,1,0:T(8,128)(2,1)S(1)}, bf16[3,64,512]{2,1,0:T(8,128)(2,1)S(1)}, u32[]{:S(2)}, u32[]{:S(2)}) collective-permute-start(bf16[3,64,512]{2,1,0:T(8,128)(2,1)S(1)} %collective-permute-done.8.refs_13_), channel_id=1, source_target_pairs={{0,224},{1,225},{2,226},{3,227},{4,228},{5,229},{6,230},{7,231},{8... | collective-permute-start | bytes 589832 | tf_op jit(solution)/shard_map/ppermute | solution.py:26
  37.4 22.4 %copy-start.5 = (bf16[3,64,512]{2,1,0:T(8,128)(2,1)}, bf16[3,64,512]{2,1,0:T(8,128)(2,1)S(1)}, u32[]{:S(2)}) copy-start(bf16[3,64,512]{2,1,0:T(8,128)(2,1)S(1)} %collective-permute-done.5.refs_20_) | copy-start | bytes 589828
  37.4 8.2 %collective-permute-start.9 = (bf16[3,64,512]{2,1,0:T(8,128)(2,1)S(1)}, bf16[3,64,512]{2,1,0:T(8,128)(2,1)S(1)}, u32[]{:S(2)}, u32[]{:S(2)}) collective-permute-start(bf16[3,64,512]{2,1,0:T(8,128)(2,1)S(1)} %collective-permute-done.8.refs_13_), channel_id=1, source_target_pairs={{0,1},{1,0},{2,3},{3,2},{4,5},{5,4},{6,7},{7,6},{8,9},{9,8},{10,11... | collective-permute-start | bytes 589832 | tf_op jit(solution)/shard_map/ppermute | solution.py:26
  41.4 18.4 %copy-start.6 = (bf16[3,64,512]{2,1,0:T(8,128)(2,1)}, bf16[3,64,512]{2,1,0:T(8,128)(2,1)S(1)}, u32[]{:S(2)}) copy-start(bf16[3,64,512]{2,1,0:T(8,128)(2,1)S(1)} %collective-permute-done.4.refs_10_) | copy-start | bytes 589828
  41.4 4.2 %collective-permute-start.7 = (bf16[3,64,512]{2,1,0:T(8,128)(2,1)S(1)}, bf16[3,64,512]{2,1,0:T(8,128)(2,1)S(1)}, u32[]{:S(2)}, u32[]{:S(2)}) collective-permute-start(bf16[3,64,512]{2,1,0:T(8,128)(2,1)S(1)} %collective-permute-done.3.refs_11_), channel_id=1, source_target_pairs={{0,1},{1,0},{2,3},{3,2},{4,5},{5,4},{6,7},{7,6},{8,9},{9,8},{10,11... | collective-permute-start | bytes 589832 | tf_op jit(solution)/shard_map/ppermute | solution.py:26
  41.4 16.5 %copy-start.18 = (bf16[3,64,512]{2,1,0:T(8,128)(2,1)}, bf16[3,64,512]{2,1,0:T(8,128)(2,1)S(1)}, u32[]{:S(2)}) copy-start(bf16[3,64,512]{2,1,0:T(8,128)(2,1)S(1)} %collective-permute-done.11.refs_2_) | copy-start | bytes 589828
  41.4 8.6 %collective-permute-start.6 = (bf16[3,64,512]{2,1,0:T(8,128)(2,1)S(1)}, bf16[3,64,512]{2,1,0:T(8,128)(2,1)}, u32[]{:S(2)}, u32[]{:S(2)}) collective-permute-start(bf16[3,64,512]{2,1,0:T(8,128)(2,1)S(1)} %collective-permute-done.4.refs_10_), channel_id=1, source_target_pairs={{0,32},{1,33},{2,34},{3,35},{4,36},{5,37},{6,38},{7,39},{8,40},{9,... | collective-permute-start | bytes 589832 | tf_op jit(solution)/shard_map/ppermute | solution.py:26
  41.9 17.9 %copy-start.7 = (bf16[3,64,512]{2,1,0:T(8,128)(2,1)}, bf16[3,64,512]{2,1,0:T(8,128)(2,1)S(1)}, u32[]{:S(2)}) copy-start(bf16[3,64,512]{2,1,0:T(8,128)(2,1)S(1)} %collective-permute-done.13.refs_14_) | copy-start | bytes 589828
  41.9 8.9 %collective-permute-start.14 = (bf16[3,64,512]{2,1,0:T(8,128)(2,1)S(1)}, bf16[3,64,512]{2,1,0:T(8,128)(2,1)}, u32[]{:S(2)}, u32[]{:S(2)}) collective-permute-start(bf16[3,64,512]{2,1,0:T(8,128)(2,1)S(1)} %collective-permute-done.13.refs_14_), channel_id=1, source_target_pairs={{0,224},{1,225},{2,226},{3,227},{4,228},{5,229},{6,230},{7,231},{8... | collective-permute-start | bytes 589832 | tf_op jit(solution)/shard_map/ppermute | solution.py:26
  45.6 5.6 %copy-start.9 = (bf16[3,64,512]{2,1,0:T(8,128)(2,1)}, bf16[3,64,512]{2,1,0:T(8,128)(2,1)S(1)}, u32[]{:S(2)}) copy-start(bf16[3,64,512]{2,1,0:T(8,128)(2,1)S(1)} %collective-permute-done.7.refs_19_) | copy-start | bytes 589828
  50.0 9.7 %copy-start = (bf16[4,4,96,768]{3,2,1,0:T(8,128)(2,1)}, bf16[4,4,96,768]{3,2,1,0:T(8,128)(2,1)S(1)}, u32[]{:S(2)}) copy-start(bf16[4,4,96,768]{3,2,1,0:T(8,128)(2,1)S(1)} %collective-permute-done.10.refs_4_.refs_5_.refs_6_.refs_7_) | copy-start | bytes 7077892
  50.0 7.9 %collective-permute-start.12 = (bf16[3,64,512]{2,1,0:T(8,128)(2,1)}, bf16[3,64,512]{2,1,0:T(8,128)(2,1)}, u32[]{:S(2)}, u32[]{:S(2)}) collective-permute-start(bf16[3,64,512]{2,1,0:T(8,128)(2,1)} %collective-permute-done.6.refs_9_), channel_id=1, source_target_pairs={{0,32},{1,33},{2,34},{3,35},{4,36},{5,37},{6,38},{7,39},{8,40},{9,... | collective-permute-start | bytes 589832 | tf_op jit(solution)/shard_map/ppermute | solution.py:26
  50.0 8.5 %collective-permute-start.18 = (bf16[3,64,512]{2,1,0:T(8,128)(2,1)S(1)}, bf16[3,64,512]{2,1,0:T(8,128)(2,1)}, u32[]{:S(2)}, u32[]{:S(2)}) collective-permute-start(bf16[3,64,512]{2,1,0:T(8,128)(2,1)S(1)} %collective-permute-done.13.refs_14_), channel_id=1, source_target_pairs={{0,1},{1,0},{2,3},{3,2},{4,5},{5,4},{6,7},{7,6},{8,9},{9,8},{10,11... | collective-permute-start | bytes 589832 | tf_op jit(solution)/shard_map/ppermute | solution.py:26
  50.1 8.4 %collective-permute-start.17 = (bf16[3,64,512]{2,1,0:T(8,128)(2,1)S(1)}, bf16[3,64,512]{2,1,0:T(8,128)(2,1)}, u32[]{:S(2)}, u32[]{:S(2)}) collective-permute-start(bf16[3,64,512]{2,1,0:T(8,128)(2,1)S(1)} %collective-permute-done.4.refs_10_), channel_id=1, source_target_pairs={{0,1},{1,0},{2,3},{3,2},{4,5},{5,4},{6,7},{7,6},{8,9},{9,8},{10,11... | collective-permute-start | bytes 589832 | tf_op jit(solution)/shard_map/ppermute | solution.py:26
  50.6 7.9 %collective-permute-start.16 = (bf16[3,64,512]{2,1,0:T(8,128)(2,1)}, bf16[3,64,512]{2,1,0:T(8,128)(2,1)}, u32[]{:S(2)}, u32[]{:S(2)}) collective-permute-start(bf16[3,64,512]{2,1,0:T(8,128)(2,1)} %collective-permute-done.6.refs_9_), channel_id=1, source_target_pairs={{0,1},{1,0},{2,3},{3,2},{4,5},{5,4},{6,7},{7,6},{8,9},{9,8},{10,11... | collective-permute-start | bytes 589832 | tf_op jit(solution)/shard_map/ppermute | solution.py:26
  50.8 7.8 %collective-permute-start.19 = (bf16[3,64,512]{2,1,0:T(8,128)(2,1)}, bf16[3,64,512]{2,1,0:T(8,128)(2,1)}, u32[]{:S(2)}, u32[]{:S(2)}) collective-permute-start(bf16[3,64,512]{2,1,0:T(8,128)(2,1)} %collective-permute-done.14.refs_15_), channel_id=1, source_target_pairs={{0,1},{1,0},{2,3},{3,2},{4,5},{5,4},{6,7},{7,6},{8,9},{9,8},{10,11... | collective-permute-start | bytes 589832 | tf_op jit(solution)/shard_map/ppermute | solution.py:26
  57.9 1.8 collective-permute-start.15
  66.0 17.8 %collective-permute-start.25 = (f32[4,96,768]{2,1,0:T(8,128)}, f32[4,96,768]{2,1,0:T(8,128)}, u32[]{:S(2)}, u32[]{:S(2)}) collective-permute-start(f32[4,96,768]{2,1,0:T(8,128)} %get-tuple-element.71), channel_id=1, source_target_pairs={{0,2},{1,9},{2,4},{3,11},{4,6},{5,13},{6,0},{7,15},{8,10},{9,17},{... | collective-permute-start | bytes 3538952 | tf_op jit(solution)/shard_map/ppermute | solution.py:26
  66.2 20.5 %collective-permute-start.22 = (f32[4,96,768]{2,1,0:T(8,128)}, f32[4,96,768]{2,1,0:T(8,128)S(1)}, u32[]{:S(2)}, u32[]{:S(2)}) collective-permute-start(f32[4,96,768]{2,1,0:T(8,128)} %get-tuple-element.56), channel_id=1, source_target_pairs={{0,6},{1,25},{2,0},{3,27},{4,2},{5,29},{6,4},{7,31},{8,14},{9,1},{... | collective-permute-start | bytes 3538952 | tf_op jit(solution)/shard_map/ppermute | solution.py:26
  79.4 23.5 %collective-permute-start.20 = (f32[4,96,768]{2,1,0:T(8,128)}, f32[4,96,768]{2,1,0:T(8,128)S(1)}, u32[]{:S(2)}, u32[]{:S(2)}) collective-permute-start(f32[4,96,768]{2,1,0:T(8,128)} %get-tuple-element.61), channel_id=1, source_target_pairs={{0,2},{1,9},{2,4},{3,11},{4,6},{5,13},{6,0},{7,15},{8,10},{9,17},{... | collective-permute-start | bytes 3538952 | tf_op jit(solution)/shard_map/ppermute | solution.py:26
  79.5 25.0 %collective-permute-start.24 = (f32[4,96,768]{2,1,0:T(8,128)}, f32[4,96,768]{2,1,0:T(8,128)S(1)}, u32[]{:S(2)}, u32[]{:S(2)}) collective-permute-start(f32[4,96,768]{2,1,0:T(8,128)} %get-tuple-element.69), channel_id=1, source_target_pairs={{0,6},{1,25},{2,0},{3,27},{4,2},{5,29},{6,4},{7,31},{8,14},{9,1},{... | collective-permute-start | bytes 3538952 | tf_op jit(solution)/shard_map/ppermute | solution.py:26
  86.7 23.1 %collective-permute-start.26 = (f32[4,96,768]{2,1,0:T(8,128)}, f32[4,96,768]{2,1,0:T(8,128)}, u32[]{:S(2)}, u32[]{:S(2)}) collective-permute-start(f32[4,96,768]{2,1,0:T(8,128)} %add.128), channel_id=1, source_target_pairs={{0,2},{1,9},{2,4},{3,11},{4,6},{5,13},{6,0},{7,15},{8,10},{9,17},{... | collective-permute-start | bytes 3538952 | tf_op jit(solution)/shard_map/ppermute | solution.py:26
  87.9 22.9 %collective-permute-start.23 = (f32[4,96,768]{2,1,0:T(8,128)}, f32[4,96,768]{2,1,0:T(8,128)}, u32[]{:S(2)}, u32[]{:S(2)}) collective-permute-start(f32[4,96,768]{2,1,0:T(8,128)} %add.124), channel_id=1, source_target_pairs={{0,6},{1,25},{2,0},{3,27},{4,2},{5,29},{6,4},{7,31},{8,14},{9,1},{... | collective-permute-start | bytes 3538952 | tf_op jit(solution)/shard_map/ppermute | solution.py:26
  99.5 2.5 %collective-permute-start.21 = (bf16[4,3,64,512]{3,2,1,0:T(8,128)(2,1)}, bf16[4,3,64,512]{3,2,1,0:T(8,128)(2,1)S(1)}, u32[]{:S(2)}, u32[]{:S(2)}) collective-permute-start(bf16[4,3,64,512]{3,2,1,0:T(8,128)(2,1)} %shard_map.79.refs_4_), channel_id=1, source_target_pairs={{0,1},{1,0},{2,3},{3,2},{4,5},{5,4},{6,7},{7,6},{8,9},{9,8},{10,11... | collective-permute-start | bytes 2359304 | tf_op jit(solution)/shard_map/ppermute | solution.py:26
  111.8 7.1 %collective-permute-start.28 = (f32[96,768]{1,0:T(8,128)S(1)}, f32[96,768]{1,0:T(8,128)}, u32[]{:S(2)}, u32[]{:S(2)}) collective-permute-start(f32[96,768]{1,0:T(8,128)S(1)} %add_bitcast_fusion.5), channel_id=1, source_target_pairs={{0,24},{1,7},{2,26},{3,1},{4,28},{5,3},{6,30},{7,5},{8,0},{9,15},{... | collective-permute-start | bytes 884744 | tf_op jit(solution)/shard_map/ppermute | solution.py:26
  114.1 9.0 %collective-permute-start.31 = (f32[96,768]{1,0:T(8,128)S(1)}, f32[96,768]{1,0:T(8,128)}, u32[]{:S(2)}, u32[]{:S(2)}) collective-permute-start(f32[96,768]{1,0:T(8,128)S(1)} %add_bitcast_fusion.4), channel_id=1, source_target_pairs={{0,8},{1,3},{2,10},{3,5},{4,12},{5,7},{6,14},{7,1},{8,16},{9,11},{... | collective-permute-start | bytes 884744 | tf_op jit(solution)/shard_map/ppermute | solution.py:26
  116.2 12.1 %collective-permute-start.27 = (f32[96,768]{1,0:T(8,128)}, f32[96,768]{1,0:T(8,128)S(1)}, u32[]{:S(2)}, u32[]{:S(2)}) collective-permute-start(f32[96,768]{1,0:T(8,128)} %get-tuple-element.74), channel_id=1, source_target_pairs={{0,8},{1,3},{2,10},{3,5},{4,12},{5,7},{6,14},{7,1},{8,16},{9,11},{... | collective-permute-start | bytes 884744 | tf_op jit(solution)/shard_map/ppermute | solution.py:26
  118.1 10.2 %collective-permute-start.30 = (f32[96,768]{1,0:T(8,128)}, f32[96,768]{1,0:T(8,128)S(1)}, u32[]{:S(2)}, u32[]{:S(2)}) collective-permute-start(f32[96,768]{1,0:T(8,128)} %get-tuple-element.76), channel_id=1, source_target_pairs={{0,24},{1,7},{2,26},{3,1},{4,28},{5,3},{6,30},{7,5},{8,0},{9,15},{... | collective-permute-start | bytes 884744 | tf_op jit(solution)/shard_map/ppermute | solution.py:26
  120.8 7.6 %collective-permute-start.29 = (f32[96,768]{1,0:T(8,128)}, f32[96,768]{1,0:T(8,128)S(1)}, u32[]{:S(2)}, u32[]{:S(2)}) collective-permute-start(f32[96,768]{1,0:T(8,128)} %bitcast_add_fusion.1), channel_id=1, source_target_pairs={{0,24},{1,7},{2,26},{3,1},{4,28},{5,3},{6,30},{7,5},{8,0},{9,15},{... | collective-permute-start | bytes 884744 | tf_op jit(solution)/shard_map/ppermute | solution.py:26
  124.9 6.9 %collective-permute-start.32 = (f32[96,768]{1,0:T(8,128)}, f32[96,768]{1,0:T(8,128)S(1)}, u32[]{:S(2)}, u32[]{:S(2)}) collective-permute-start(f32[96,768]{1,0:T(8,128)} %bitcast_add_fusion), channel_id=1, source_target_pairs={{0,8},{1,3},{2,10},{3,5},{4,12},{5,7},{6,14},{7,1},{8,16},{9,11},{... | collective-permute-start | bytes 884744 | tf_op jit(solution)/shard_map/ppermute | solution.py:26
  135.8 6.6 %collective-permute-start.33 = (f32[3,96,128]{2,1,0:T(8,128)}, f32[3,96,128]{2,1,0:T(8,128)S(1)}, u32[]{:S(2)}, u32[]{:S(2)}) collective-permute-start(f32[3,96,128]{2,1,0:T(8,128)} %get-tuple-element.80), channel_id=1, source_target_pairs={{0,2},{1,3},{2,4},{3,5},{4,6},{5,7},{6,0},{7,1},{8,10},{9,11},{10,... | collective-permute-start | bytes 442376 | tf_op jit(solution)/shard_map/ppermute | solution.py:26
  136.1 8.3 %collective-permute-start.34 = (f32[3,96,128]{2,1,0:T(8,128)}, f32[3,96,128]{2,1,0:T(8,128)S(1)}, u32[]{:S(2)}, u32[]{:S(2)}) collective-permute-start(f32[3,96,128]{2,1,0:T(8,128)} %get-tuple-element.81), channel_id=1, source_target_pairs={{0,4},{1,5},{2,6},{3,7},{4,0},{5,1},{6,2},{7,3},{8,12},{9,13},{10,... | collective-permute-start | bytes 442376 | tf_op jit(solution)/shard_map/ppermute | solution.py:26
  139.5 5.4 %collective-permute-start.35 = (f32[3,96,128]{2,1,0:T(8,128)}, f32[3,96,128]{2,1,0:T(8,128)S(1)}, u32[]{:S(2)}, u32[]{:S(2)}) collective-permute-start(f32[3,96,128]{2,1,0:T(8,128)} %get-tuple-element.82), channel_id=1, source_target_pairs={{0,6},{1,7},{2,0},{3,1},{4,2},{5,3},{6,4},{7,5},{8,14},{9,15},{10,... | collective-permute-start | bytes 442376 | tf_op jit(solution)/shard_map/ppermute | solution.py:26
  149.4 2.3 collective-permute-start.36
  234.0 5.0 %collective-permute-start.37 = (f32[16,8,5,8,128]{4,3,2,1,0:T(8,128)S(1)}, f32[16,8,5,8,128]{4,3,2,1,0:T(8,128)}, u32[]{:S(2)}, u32[]{:S(2)}) collective-permute-start(f32[16,8,5,8,128]{4,3,2,1,0:T(8,128)S(1)} %all_to_all.23.plane), channel_id=1, source_target_pairs={{0,1},{1,0},{2,3},{3,2},{4,5},{5,4},{6,7},{7,6},{8,9},{9,8},{10,11... | collective-permute-start | bytes 7864328 | tf_op jit(solution)/shard_map/ppermute | solution.py:26
  (12 other events, 30.7 us)
